TPU v7x, 128 devices: a whole 4x4x4 slice. The times are simulated.
128 devices in a mesh: wafer: 4 (over z), det: 32 (over y, x, core).
Axes of the slice: x: 4, y: 4, z: 4, core: 2. Of those that a mesh axis runs over, the one named last changes fastest.
Arguments:
- tod: float32 [8192, 8192], P(('wafer', 'det')), may hold values from -12 to 12
- gap_mask: int32 [8192, 8192], P(('wafer', 'det')), may hold values from 0 to 1
- coupling: float32 [8192, 32], P(('wafer', 'det')), may hold values from -5 to 5
- taps: float32 [129], replicated, may hold values from -1 to 1
- cross_det: int32 [8192], P(('wafer', 'det')), may hold values from 0 to 63
- cross_start: int32 [8192], P(('wafer', 'det')), may hold values from 0 to 7936
- cross_src: int32 [8192], P(('wafer', 'det')), may hold values from 0 to 127, as said below
- src_owner: int32 [128], replicated, may hold values from 0 to 127, as said below
Outputs:
- filled: float32 [8192, 8192], P(('wafer', 'det'))
- templates: float32 [4, 128, 256], P('wafer', 'det')
Inputs may be any that keep to these rules, and one draw needn't show every extreme that they name: src_owner is a permutation of the template slots. `cross_src`: among one device's 64 crossings, at most 4 have slots in one block of 4 slots (o // 4 equal); in every device some block gets exactly 4.
All inputs are finite; a program needn't handle non-finite values.
Results may differ from a plain program's by a relative error of at most 0.00014.
Values sent between devices are 32-bit elements; how exact they have to be, the bound alone decides.
A program may use at most 64 MiB of HBM per device.

v0:
```python
import jax
import jax.numpy as jnp
from jax import lax
from jax.sharding import PartitionSpec as P

SNIP = 256
SRC_DEV = 4


def correlate(resid, taps):
    highest = lax.Precision.HIGHEST
    n_taps = taps.shape[0]
    half = (n_taps - 1) // 2
    width = 128
    rows_in = jnp.arange(2 * width, dtype=jnp.int32)[:, None]
    cols_out = jnp.arange(width, dtype=jnp.int32)[None, :]
    offset = rows_in - cols_out
    inside = (offset >= 0) & (offset < n_taps)
    band = jnp.where(inside, jnp.take(taps, jnp.clip(offset, 0, n_taps - 1)), 0.0)
    n_rows, n_samples = resid.shape
    n_blocks = n_samples // width
    padded = jnp.pad(resid, ((0, 0), (half, width - half)))
    blocks = padded.reshape(n_rows, n_blocks + 1, width)
    upper = jnp.einsum("rbi,ij->rbj", blocks[:, :n_blocks, :], band[:width], precision=highest)
    lower = jnp.einsum("rbi,ij->rbj", blocks[:, 1:, :], band[width:], precision=highest)
    return (upper + lower).reshape(n_rows, n_samples)


def on_device(tod, gap_mask, coupling, taps, cross_det, cross_start, cross_src, src_owner):
    highest = lax.Precision.HIGHEST
    good = gap_mask.astype(jnp.float32)
    part_sum = jnp.dot(coupling.T, good * tod, precision=highest)
    part_weight = jnp.dot((coupling * coupling).T, good, precision=highest)
    whole_sum, whole_weight = lax.psum((part_sum, part_weight), ("wafer", "det"))
    amplitude = whole_sum / (whole_weight + 1.0)
    model = jnp.dot(coupling, amplitude, precision=highest)
    resid = good * (tod - model)
    smooth = correlate(resid, taps)
    filled = good * tod + (1.0 - good) * (model + smooth)
    snip_len = SNIP
    columns = cross_start[:, None] + jnp.arange(snip_len, dtype=jnp.int32)[None, :]
    snippet = resid[cross_det[:, None], columns]
    owned = src_owner[cross_src]
    n_det = lax.axis_size("det")
    n_cross = cross_det.shape[0]
    src_local = SRC_DEV
    labels = (jnp.arange(src_local, dtype=jnp.int32) + 1).astype(jnp.float32)
    capacity = 2 * n_cross // n_det
    target = owned // src_local
    onehot = (target[:, None] == jnp.arange(n_det, dtype=jnp.int32)[None, :]).astype(jnp.int32)
    before = jnp.cumsum(onehot, axis=0) - onehot
    rank = jnp.sum(before * onehot, axis=1)
    position = target * capacity + rank
    send_rows = jnp.zeros((n_det * capacity, snip_len), jnp.float32).at[position].set(snippet)
    send_ids = (
        jnp.zeros((n_det * capacity,), jnp.float32)
        .at[position]
        .set((owned % src_local + 1).astype(jnp.float32))
    )
    got_rows, got_ids = (
        lax.all_to_all(
            send_rows.reshape(n_det, capacity, snip_len),
            "det",
            split_axis=0,
            concat_axis=0,
            tiled=True,
        ),
        lax.all_to_all(
            send_ids.reshape(n_det, capacity), "det", split_axis=0, concat_axis=0, tiled=True
        ),
    )
    got_rows = got_rows.reshape(n_det * capacity, snip_len)
    got_ids = got_ids.reshape(n_det * capacity)
    select = (got_ids[:, None] == labels[None, :]).astype(jnp.float32)
    sums = jnp.dot(select.T, got_rows, precision=highest)
    counts = jnp.sum(select, axis=0)
    templates = (sums / (counts + 1.0)[:, None])[None, :, :]
    return (filled, templates)


def solution(mesh):
    return jax.shard_map(
        on_device,
        mesh=mesh,
        in_specs=(
            P(("wafer", "det"), None),
            P(("wafer", "det"), None),
            P(("wafer", "det"), None),
            P(),
            P(("wafer", "det")),
            P(("wafer", "det")),
            P(("wafer", "det")),
            P(),
        ),
        out_specs=(P(("wafer", "det"), None), P("wafer", "det", None)),
        check_vma=False,
    )
```

profile of v0, /device:TPU:1, one launch (start us, length us, event | category | flops | bytes accessed | tf_op | source)
XLA Modules:
  0.0 396.7 jit_solution(122100362077766414)
XLA Ops:
  7.2 0.8 compare_select_fusion.5
  8.0 1.4 gather_fusion.1
  9.8 0.8 scatter_custom_fusion
  10.6 0.7 all_to_all.9
  11.3 8.6 %all-to-all-start = ((f32[32,1,4]{2,1,0:T(1,128)}), f32[32,1,4]{2,1,0:T(1,128)S(1)}, u32[]{:S(2)}, u32[]{:S(2)}) async-start(f32[32,1,4]{2,1,0:T(1,128)} %bitcast.9), calls=%async_computation | async-start | bytes 32768 | tf_op jit(solution)/shard_map/all_to_all | solution.py:68
  20.0 3.8 fusion.6
  23.7 4.0 %convolution_bitcast_fusion.1 = f32[32,8192]{1,0:T(8,128)} fusion(f32[64,32]{0,1:T(8,128)S(1)} %copy-done.5, f32[64,8192]{1,0:T(8,128)} %param.8, s32[64,8192]{1,0:T(8,128)S(1)} %copy-done.1), kind=kOutput, calls=%fused_computation.6 | convolution fusion | flops 202375168 | bytes 5251072 | tf_op jit(solution)/shard_map/dot_general | solution.py:32
  27.8 203.2 %gather_fusion = f32[32768]{0:T(1024)S(1)} fusion(f32[129]{0:T(256)S(1)} %copy-done, s32[32768]{0:T(1024)S(1)} %fusion.16), kind=kCustom, calls=%fused_computation | custom fusion | bytes 393216 | tf_op jit(solution)/shard_map/jit(_take)/gather | solution.py:19
  231.3 0.5 broadcast.286
  231.8 0.7 reduce.3
  232.6 0.2 fusion.33
  232.8 6.3 %subtract_multiply_fusion = (f32[64,8192]{1,0:T(8,128)S(1)}, f32[64,8192]{1,0:T(8,128)}) fusion(f32[64,8192]{1,0:T(8,128)} %param.8, s32[64,8192]{1,0:T(8,128)} %param.9, f32[64,32]{0,1:T(8,128)S(1)} %copy-done.5, f32[32,8192]{1,0:T(8,128)} %get-tuple-element.2, f32[32,8192]{1,0:T(8,128)} %get-tuple-element.3), kind=kOutput, calls=%fused_computation.14 | convolution fusion | flops 203423744 | bytes 10493952 | tf_op jit(solution)/shard_map/dot_general | solution.py:36
  239.1 2.0 pad.4
  241.1 129.5 %gather_fusion.2 = f32[16384]{0:T(1024)S(1)} fusion(f32[64,8192]{1,0:T(8,128)S(1)} %get-tuple-element.6, s32[16384]{0:T(1024)S(1)} %bitcast.51), kind=kCustom, calls=%fused_computation.2 | custom fusion | bytes 262144 | tf_op jit(solution)/shard_map/gather | solution.py:42
  370.6 0.8 scatter_custom_fusion.1
  371.4 0.7 reshape.189
  372.1 7.4 %all-to-all-start.1 = ((f32[32,4,256]{2,1,0:T(4,128)}), f32[32,4,256]{2,1,0:T(4,128)S(1)}, u32[]{:S(2)}, u32[]{:S(2)}) async-start(f32[32,4,256]{2,1,0:T(4,128)} %reshape.189), calls=%async_computation.1 | async-start | bytes 262144 | tf_op jit(solution)/shard_map/all_to_all | solution.py:61
  379.5 1.7 reshape.187
  381.3 1.8 fusion.2
  383.1 1.8 fusion.8
  384.9 0.4 copy-done.3
  385.3 0.6 copy-done.4
  385.9 3.0 fusion.1
  389.0 0.8 fusion.11
  (35 shorter events, 1.0 us)
Async XLA Ops:
  7.2 20.6 %copy-start = (f32[129]{0:T(256)S(1)}, f32[129]{0:T(256)}, u32[]{:S(2)}) copy-start(f32[129]{0:T(256)} %param.11) | copy-start | bytes 1552
  7.2 16.6 %copy-start.5 = (f32[64,32]{0,1:T(8,128)S(1)}, f32[64,32]{0,1:T(8,128)}, u32[]{:S(2)}) copy-start(f32[64,32]{0,1:T(8,128)} %param.10) | copy-start | bytes 24580
  7.2 16.5 %copy-start.1 = (s32[64,8192]{1,0:T(8,128)S(1)}, s32[64,8192]{1,0:T(8,128)}, u32[]{:S(2)}) copy-start(s32[64,8192]{1,0:T(8,128)} %param.9) | copy-start | bytes 6291460
  11.3 220.0 %all-to-all-start = ((f32[32,1,4]{2,1,0:T(1,128)}), f32[32,1,4]{2,1,0:T(1,128)S(1)}, u32[]{:S(2)}, u32[]{:S(2)}) async-start(f32[32,1,4]{2,1,0:T(1,128)} %bitcast.9), calls=%async_computation | async-start | bytes 32768 | tf_op jit(solution)/shard_map/all_to_all | solution.py:68
  19.9 212.9 %all-reduce.4.cloned.1.call-start = ((), (), s32[]{:S(2)}) async-start(), calls=%async_computation.2 | async-start | bytes 4194304 | tf_op jit(solution)/shard_map/psum | solution.py:34
  27.8 203.2 %copy-start.7 = (s32[64]{0:T(128)S(1)}, s32[64]{0:T(128)}, u32[]{:S(2)}) copy-start(s32[64]{0:T(128)} %param.12) | copy-start | bytes 772
  27.8 203.2 %copy-start.6 = (s32[64]{0:T(128)S(1)}, s32[64]{0:T(128)}, u32[]{:S(2)}) copy-start(s32[64]{0:T(128)} %param.13) | copy-start | bytes 772
  372.1 16.8 %all-to-all-start.1 = ((f32[32,4,256]{2,1,0:T(4,128)}), f32[32,4,256]{2,1,0:T(4,128)S(1)}, u32[]{:S(2)}, u32[]{:S(2)}) async-start(f32[32,4,256]{2,1,0:T(4,128)} %reshape.189), calls=%async_computation.1 | async-start | bytes 262144 | tf_op jit(solution)/shard_map/all_to_all | solution.py:61
  383.0 1.8 copy-start.2
  383.1 2.2 copy-start.3
  383.1 2.8 copy-start.4
Sparse Core Ops, SparseCore 0:
  27.9 153.1 all-reduce.3
where the time goes:
time: 397 us
  local copies, waits for them, and re-layouts  343 us (86%)
  matrix products  18.4 us (5%)
  starting transfers between devices  16 us (4%)
  between operations  14.3 us (4%)
  other arithmetic  5.34 us (1%)
    gather x1, local copies, waits for them, and re-layouts, correlate(): jnp.take(taps, jnp.clip(offset, 0, n_taps - 1))  203 us
    gather x2, local copies, waits for them, and re-layouts, on_device(): snippet = resid[cross_det[:, None], columns]  129 us
    all_to_all x1, starting transfers between devices, on_device(): lax.all_to_all(send_ids.reshape(n_det, capacity), 'det', split_axis=0, co...  8.58 us
  transfers between devices with their start and end apart: 3, of which 0 were waited for; matrix products, arithmetic and copies ran while one was open for 56% of the time, Pallas kernels for 0%

commit v1 on v0

v1 whole, which is shorter than its diff:
```python
import functools

import jax
import jax.numpy as jnp
from jax import lax
from jax.experimental import pallas as pl
from jax.experimental.pallas import tpu as pltpu
from jax.sharding import PartitionSpec as P

MESH = pl.DeviceIdType.MESH
F32 = jnp.float32
BF16 = jnp.bfloat16

ROWS = 64
NS = 8192
HALF = NS // 2
MODES = 32
TAPS = 129
CROSS = 64
RING = 4
DET = 32
SETS = (
    (0, 384, ("x", "y", "z")),
    (1536, 384, ("y", "z", "x")),
    (3072, 256, ("z", "x", "y")),
)
PLACE = (0, 384, 768)
BLOCKS = 1024


def split(v):
    hi = v.astype(BF16)
    lo = (v - hi.astype(F32)).astype(BF16)
    return hi, lo


def dot(a, b):
    return jnp.dot(a, b, preferred_element_type=F32)


def kernel(
    tod_hbm, mask_hbm, coup_ref, taps_ref, cdet_ref, cstart_ref, csrc_ref, owner_ref,
    filled_ref, templ_ref,
    tod, mask, model, res_hi, res_lo,
    part, acc, got_c, got1, acc1, got2, acc2, got3, amp,
    lhs_p, lhs_m, band,
    slots, dets, first_tile, shift, snip, cnt, cnt_got, tsum, tsum_got,
    in_sem, c_sem, r_sem, g_sem, gc_sem, t_sem,
):
    wafer = lax.axis_index("wafer")
    det = lax.axis_index("det")
    core = lax.rem(det, 2)
    x = lax.rem(lax.div(det, 2), RING)
    y = lax.div(det, 2 * RING)
    coord = {"x": x, "y": y, "z": wafer}

    def along(axis, step):
        xx, yy, zz = x, y, wafer
        if axis == "x":
            xx = lax.rem(x + step, RING)
        elif axis == "y":
            yy = lax.rem(y + step, RING)
        else:
            zz = lax.rem(wafer + step, RING)
        return (zz, (yy * RING + xx) * 2 + core)

    partner = (wafer, det + 1 - 2 * core)

    def remote(src, dst, send, recv, to):
        return pltpu.make_async_remote_copy(
            src_ref=src, dst_ref=dst, send_sem=send, recv_sem=recv,
            device_id=to, device_id_type=MESH,
        )

    def cols(first, width):
        return pl.ds(pl.multiple_of(first, 128), width)

    halves = (1 - core, core)
    loads = []
    for h in range(2):
        for s, (base, width, _) in enumerate(SETS):
            span = cols(halves[h] * HALF + base, RING * width)
            pair = (
                pltpu.make_async_copy(tod_hbm.at[:, span], tod.at[:, span], in_sem.at[h, s, 0]),
                pltpu.make_async_copy(mask_hbm.at[:, span], mask.at[:, span], in_sem.at[h, s, 1]),
            )
            for one in pair:
                one.start()
            loads.append(pair)

    barrier = pltpu.get_barrier_semaphore()
    for step in range(1, DET):
        pl.semaphore_signal(
            barrier, inc=1, device_id=(wafer, lax.rem(det + step, DET)), device_id_type=MESH
        )
    for step in range(1, RING):
        pl.semaphore_signal(barrier, inc=1, device_id=along("z", step), device_id_type=MESH)

    coup_t = coup_ref[...]
    c_hi, c_lo = split(coup_t.T)
    lhs_m[...] = jnp.concatenate([c_hi, c_lo, c_hi], axis=1)
    t_hi, t_lo = split(coup_t)
    w_hi, w_lo = split(coup_t * coup_t)
    zero = jnp.zeros((MODES, ROWS), BF16)
    lhs_p[0:32, :] = jnp.concatenate([t_hi, t_lo, t_hi, zero], axis=1)
    lhs_p[32:64, :] = jnp.concatenate([zero, zero, zero, w_hi], axis=1)
    lhs_p[64:96, :] = jnp.concatenate([zero, zero, zero, w_lo], axis=1)

    def partial_sums(first, width):
        span = cols(first, width)
        m = mask[:, span]
        v = jnp.where(m != 0, tod[:, span], 0.0)
        v_hi, v_lo = split(v)
        g = m.astype(F32).astype(BF16)
        out = dot(lhs_p[...], jnp.concatenate([v_hi, v_hi, v_lo, g], axis=0))
        return out[0:32], out[32:64] + out[64:96]

    def fill(h, s, dst):
        base, width, _ = SETS[s]
        for one in loads[h * 3 + s]:
            one.wait()

        def body(i, carry):
            local = base + i * width
            sums, weights = partial_sums(halves[h] * HALF + local, width)
            span = cols(local, width)
            for j in range(RING):
                dst[j, 0:8, span] = sums[8 * j:8 * j + 8]
                dst[j, 8:16, span] = weights[8 * j:8 * j + 8]
            return carry

        lax.fori_loop(0, RING, body, 0)

    copies_c = []
    for s, (base, width, _) in enumerate(SETS):
        span = pl.ds(base, RING * width)
        copies_c.append(
            remote(part.at[:, :, span], got_c.at[:, :, span], c_sem.at[s, 0], c_sem.at[s, 1], partner)
        )
    fill(0, 0, part)
    pl.semaphore_wait(barrier, DET - 1 + RING - 1)
    copies_c[0].start()
    for s in (1, 2):
        fill(0, s, part)
        copies_c[s].start()
    for s in range(3):
        fill(1, s, acc)

    owner = 2 * owner_ref[...]
    src_iota = lax.broadcasted_iota(jnp.int32, (128, CROSS), 0)
    of_src = (src_iota == csrc_ref[...]).astype(F32).astype(BF16)
    row_iota = lax.broadcasted_iota(jnp.int32, (256, 128), 0)
    perm0 = (row_iota == owner).astype(F32).astype(BF16)
    perm1 = (row_iota == owner + 1).astype(F32).astype(BF16)
    oh_t = jnp.concatenate([dot(perm0, of_src), dot(perm1, of_src)], axis=1)
    slots[:, 0:128] = oh_t.astype(BF16)
    slots[:, 128:256] = oh_t.astype(BF16)
    det_iota = lax.broadcasted_iota(jnp.int32, (ROWS, CROSS), 0)
    of_det = (det_iota == cdet_ref[...]).astype(F32).T.astype(BF16)
    dets[...] = jnp.concatenate([of_det, of_det], axis=1)
    start = jnp.broadcast_to(cstart_ref[...], (128, CROSS)).T
    first_tile[...] = start >> 7
    shift[...] = start & 127
    cnt[...] = jnp.broadcast_to(jnp.sum(oh_t, axis=1, keepdims=True), (256, 128)).reshape(DET, 8, 128)
    copies_n = []
    for step in range(1, DET):
        to = lax.rem(det + step, DET)
        copies_n.append(
            remote(cnt.at[to], cnt_got.at[step - 1], t_sem.at[0], t_sem.at[1], (wafer, to))
        )
        copies_n[-1].start()

    def exchange(sem, axis, src_of, dst_of):
        made = []
        for step in range(1, RING):
            made.append(
                remote(src_of(step), dst_of(step), sem.at[step - 1, 0], sem.at[step - 1, 1], along(axis, step))
            )
        for one in made:
            one.start()
        return made

    stage1 = []
    for s, (base, width, order) in enumerate(SETS):
        copies_c[s].wait_recv()
        span = pl.ds(base, RING * width)
        acc[:, :, span] += got_c[:, :, span]
        axis = order[0]

        def src_of(step, base=base, width=width, axis=axis):
            to = lax.rem(coord[axis] + step, RING)
            return acc.at[:, :, cols(base + to * width, width)]

        def dst_of(step, s=s, width=width):
            return got1.at[step - 1, :, :, pl.ds(PLACE[s], width)]

        stage1.append(exchange(r_sem.at[s, 0], axis, src_of, dst_of))

    row = lax.broadcasted_iota(jnp.int32, (256, 128), 0)
    col = lax.broadcasted_iota(jnp.int32, (256, 128), 1)
    pos = jnp.where(row < 192, row, row - 256)
    tap_of = pos - col + 64

    def add_tap(k, total):
        return total + jnp.where(tap_of == k, taps_ref[k], 0.0)

    b_hi, b_lo = split(lax.fori_loop(0, TAPS, add_tap, jnp.zeros((256, 128), F32)))
    band[:, 0:128] = b_hi
    band[:, 128:256] = b_lo

    stage2 = []
    for s, (base, width, order) in enumerate(SETS):
        for one in stage1[s]:
            one.wait_recv()
        mine = cols(base + coord[order[0]] * width, width)
        span = pl.ds(PLACE[s], width)
        acc1[:, :, span] = (acc[:, :, mine] + got1[0, :, :, span]) + (got1[1, :, :, span] + got1[2, :, :, span])
        axis = order[1]

        def src_of(step, span=span, axis=axis):
            return acc1.at[lax.rem(coord[axis] + step, RING), :, span]

        def dst_of(step, span=span):
            return got2.at[step - 1, :, span]

        stage2.append(exchange(r_sem.at[s, 1], axis, src_of, dst_of))

    stage3 = []
    for s, (base, width, order) in enumerate(SETS):
        for one in stage2[s]:
            one.wait_recv()
        span = pl.ds(PLACE[s], width)
        acc2[:, span] = (acc1[coord[order[1]], :, span] + got2[0, :, span]) + (got2[1, :, span] + got2[2, :, span])

        def src_of(step, span=span):
            return acc2.at[:, span]

        def dst_of(step, span=span):
            return got3.at[step - 1, :, span]

        stage3.append(exchange(r_sem.at[s, 2], order[2], src_of, dst_of))

    gather2 = []
    for s, (base, width, order) in enumerate(SETS):
        for one in stage3[s]:
            one.wait_recv()
        span = pl.ds(PLACE[s], width)
        whole = (acc2[:, span] + got3[0, :, span]) + (got3[1, :, span] + got3[2, :, span])
        block = cols(core * HALF + base + coord[order[0]] * width, width)
        amp[coord[order[1]], :, block] = whole[0:8] / (whole[8:16] + 1.0)

        def here(step, block=block, j=coord[order[1]]):
            return amp.at[j, :, block]

        gather2.append(exchange(g_sem.at[s, 0], order[1], here, here))

    gather1 = []
    for s, (base, width, order) in enumerate(SETS):
        for one in gather2[s]:
            one.wait_recv()
        block = cols(core * HALF + base + coord[order[0]] * width, width)

        def here(step, block=block):
            return amp.at[:, :, block]

        gather1.append(exchange(g_sem.at[s, 1], order[0], here, here))

    copies_a = []
    for s, (base, width, order) in enumerate(SETS):
        for one in gather1[s]:
            one.wait_recv()
        span = cols(core * HALF + base, RING * width)
        copies_a.append(remote(amp.at[:, :, span], amp.at[:, :, span], gc_sem.at[s, 0], gc_sem.at[s, 1], partner))
        copies_a[-1].start()
    for one in copies_a:
        one.wait_recv()

    for edge in (res_hi, res_lo):
        edge[:, 0:128] = jnp.zeros((ROWS, 128), BF16)
        edge[:, 128 + NS:256 + NS] = jnp.zeros((ROWS, 128), BF16)

    def model_block(b, wide):
        span = cols(b * 512, 512)
        a_hi, a_lo = split(amp[:, :, span].reshape(MODES, 512))
        value = dot(lhs_m[...], jnp.concatenate([a_hi, a_hi, a_lo], axis=0))
        model[:, span] = value
        r_hi, r_lo = split(jnp.where(mask[:, span] != 0, tod[:, span] - value, 0.0))
        res_hi[:, cols(b * 512 + 128, 512)] = r_hi
        res_lo[:, cols(b * 512 + 128, 512)] = r_lo
        lines = dot(dets[...], jnp.concatenate([r_hi, r_lo], axis=0))
        tile = first_tile[...]
        wide = list(wide)
        for q in range(4):
            for w in range(3):
                wide[w] = jnp.where(tile == b * 4 + q - w, lines[:, 128 * q:128 * q + 128], wide[w])
        return tuple(wide)

    wide = lax.fori_loop(0, NS // 512, model_block, (jnp.zeros((CROSS, 128), F32),) * 3)

    rows = jnp.concatenate(wide, axis=1)
    rest = jnp.concatenate([shift[...]] * 3, axis=1)
    for bit in range(7):
        moved = pltpu.roll(rows, 384 - (1 << bit), 1)
        rows = jnp.where((rest & (1 << bit)) != 0, moved, rows)
    snip[0:CROSS, :] = rows[:, 0:128]
    snip[CROSS:2 * CROSS, :] = rows[:, 128:256]
    s_hi, s_lo = split(snip[...])
    tsum[...] = dot(slots[...], jnp.concatenate([s_hi, s_lo], axis=0)).reshape(DET, 8, 128)
    copies_t = []
    for step in range(1, DET):
        to = lax.rem(det + step, DET)
        copies_t.append(
            remote(tsum.at[to], tsum_got.at[step - 1], t_sem.at[2], t_sem.at[3], (wafer, to))
        )
        copies_t[-1].start()

    lane64 = lax.broadcasted_iota(jnp.int32, (ROWS, 128), 1) < 64

    def fill_block(b, carry):
        pieces = []
        for res in (res_hi, res_lo):
            left = []
            for q in range(4):
                before = res[:, cols(b * 512 + q * 128, 128)]
                here = res[:, cols(b * 512 + q * 128 + 128, 128)]
                after = res[:, cols(b * 512 + q * 128 + 256, 128)]
                left.append(jnp.concatenate([here, jnp.where(lane64, after, before)], axis=1))
            pieces.append(jnp.concatenate(left, axis=0))
        l_hi, l_lo = pieces
        first = dot(l_hi, band[...])
        second = dot(l_lo, band[:, 0:128])
        smooth = first[:, 0:128] + (first[:, 128:256] + second)
        for q in range(4):
            span = cols(b * 512 + q * 128, 128)
            filled_ref[:, span] = jnp.where(
                mask[:, span] != 0, tod[:, span], model[:, span] + smooth[q * ROWS:(q + 1) * ROWS]
            )
        return carry

    lax.fori_loop(0, NS // 512, fill_block, 0)

    def wait_all(src, dst, send, recv):
        every = remote(src.at[0:DET - 1], dst.at[0:DET - 1], send, recv, partner)
        every.wait_recv()
        every.wait_send()

    wait_all(cnt, cnt_got, t_sem.at[0], t_sem.at[1])
    wait_all(tsum, tsum_got, t_sem.at[2], t_sem.at[3])
    number = cnt[det]
    total = tsum[det]
    for step in range(DET - 1):
        number += cnt_got[step]
        total += tsum_got[step]
    snip[0:8, :] = total / (number + 1.0)
    for o in range(4):
        templ_ref[0, o:o + 1, 0:128] = snip[2 * o:2 * o + 1, :]
        templ_ref[0, o:o + 1, 128:256] = snip[2 * o + 1:2 * o + 2, :]

    for one in copies_c + copies_a:
        one.wait_send()
    for group in stage1 + stage2 + stage3 + gather2 + gather1:
        for one in group:
            one.wait_send()


def on_device(tod, gap_mask, coupling, taps, cross_det, cross_start, cross_src, src_owner):
    vmem, smem, hbm = (pl.BlockSpec(memory_space=m) for m in (pltpu.VMEM, pltpu.SMEM, pltpu.HBM))
    return pl.pallas_call(
        kernel,
        out_shape=(
            jax.ShapeDtypeStruct((ROWS, NS), F32),
            jax.ShapeDtypeStruct((1, 4, 256), F32),
        ),
        in_specs=[hbm, hbm, vmem, smem, vmem, vmem, vmem, vmem],
        out_specs=(vmem, vmem),
        scratch_shapes=[
            pltpu.VMEM((ROWS, NS), F32),
            pltpu.VMEM((ROWS, NS), jnp.int32),
            pltpu.VMEM((ROWS, NS), F32),
            pltpu.VMEM((ROWS, NS + 256), BF16),
            pltpu.VMEM((ROWS, NS + 256), BF16),
            pltpu.VMEM((RING, 16, HALF), F32),
            pltpu.VMEM((RING, 16, HALF), F32),
            pltpu.VMEM((RING, 16, HALF), F32),
            pltpu.VMEM((3, RING, 16, BLOCKS), F32),
            pltpu.VMEM((RING, 16, BLOCKS), F32),
            pltpu.VMEM((3, 16, BLOCKS), F32),
            pltpu.VMEM((16, BLOCKS), F32),
            pltpu.VMEM((3, 16, BLOCKS), F32),
            pltpu.VMEM((RING, 8, NS), F32),
            pltpu.VMEM((96, 256), BF16),
            pltpu.VMEM((ROWS, 96), BF16),
            pltpu.VMEM((256, 256), BF16),
            pltpu.VMEM((256, 256), BF16),
            pltpu.VMEM((CROSS, 128), BF16),
            pltpu.VMEM((CROSS, 128), jnp.int32),
            pltpu.VMEM((CROSS, 128), jnp.int32),
            pltpu.VMEM((2 * CROSS, 128), F32),
            pltpu.VMEM((DET, 8, 128), F32),
            pltpu.VMEM((DET, 8, 128), F32),
            pltpu.VMEM((DET, 8, 128), F32),
            pltpu.VMEM((DET, 8, 128), F32),
            pltpu.SemaphoreType.DMA((2, 3, 2)),
            pltpu.SemaphoreType.DMA((3, 2)),
            pltpu.SemaphoreType.DMA((3, 3, 3, 2)),
            pltpu.SemaphoreType.DMA((3, 2, 3, 2)),
            pltpu.SemaphoreType.DMA((3, 2)),
            pltpu.SemaphoreType.DMA((4,)),
        ],
        compiler_params=pltpu.CompilerParams(
            collective_id=0, has_side_effects=True, vmem_limit_bytes=48 << 20
        ),
    )(tod, gap_mask, coupling.T, taps, *(v.reshape(1, -1) for v in (cross_det, cross_start, cross_src, src_owner)))


def solution(mesh):
    return jax.shard_map(
        on_device,
        mesh=mesh,
        in_specs=(
            P(("wafer", "det"), None),
            P(("wafer", "det"), None),
            P(("wafer", "det"), None),
            P(),
            P(("wafer", "det")),
            P(("wafer", "det")),
            P(("wafer", "det")),
            P(),
        ),
        out_specs=(P(("wafer", "det"), None), P("wafer", "det", None)),
        check_vma=False,
    )
```

time: 397 us -> 59 us (0.15)
  local copies, waits for them, and re-layouts: 343 us -> 7.51 us
  Pallas kernels: 0 us -> 50.6 us
  matrix products: 18.4 us -> 0 us
  starting transfers between devices: 16 us -> 0 us
  between operations: 14.3 us -> 0.66 us
  other arithmetic: 5.34 us -> 0 us
    gather x4 -> x0, local copies, waits for them, and re-layouts: 334 us -> none  [the longest x1 203 us: correlate(): jnp.take(taps, jnp.clip(offset, 0, n_taps - 1))]
    pallas_call x0 -> x1, Pallas kernels: none -> 50.6 us  [on_device(): pl.pallas_call(kernel, out_shape=(jax.ShapeDtypeStruct((ROWS, NS), F32),...]
    dot_general x6 -> x0, matrix products: 18.4 us -> none  [the longest x1 6.27 us: on_device(): model = jnp.dot(coupling, amplitude, precision=highest)]
    all_to_all x2 -> x0, starting transfers between devices: 16 us -> none  [the longest x1 8.58 us: on_device(): lax.all_to_all(send_ids.reshape(n_det, capacity), 'det', split_axis=0, co...]
    unnamed x17 -> x16, local copies, waits for them, and re-layouts: 1.12 us -> 7.51 us
  transfers between devices with their start and end apart: 3 -> 0, of which waited for: 0 -> 0; matrix products, arithmetic and copies ran while one was open for 56% -> 0% of each run, Pallas kernels for 0% -> 0%
where the time goes in v1:
time: 59 us; the launch traced here: 58.8 us
  Pallas kernels  50.6 us (86%)
  local copies, waits for them, and re-layouts  7.51 us (13%)
  between operations  0.66 us (1%)
    pallas_call x1, Pallas kernels, on_device(): pl.pallas_call(kernel, out_shape=(jax.ShapeDtypeStruct((ROWS, NS), F32),...  50.6 us
    unnamed x16, local copies, waits for them, and re-layouts  7.51 us

profile of v1, /device:TPU:1, one launch (start us, length us, event | category | flops | bytes accessed | tf_op | source)
XLA Modules:
  0.0 58.8 jit_solution(15452991686507309187)
XLA Ops:
  0.6 0.0 copy-start
  0.6 1.6 %copy-done = f32[64,8192]{1,0:T(8,128)S(1)} copy-done((f32[64,8192]{1,0:T(8,128)S(1)}, f32[64,8192]{1,0:T(8,128)}, u32[]{:S(2)}) %copy-start) | copy-done | bytes 2097176
  2.2 0.0 copy-start.1
  2.2 0.7 %copy-done.1 = f32[64,32]{0,1:T(8,128)S(1)} copy-done((f32[64,32]{0,1:T(8,128)S(1)}, f32[64,32]{0,1:T(8,128)}, u32[]{:S(2)}) %copy-start.1) | copy-done | bytes 8216
  2.9 0.0 copy-start.2
  2.9 0.7 %copy-done.2 = f32[129]{0:T(256)S(1)} copy-done((f32[129]{0:T(256)S(1)}, f32[129]{0:T(256)}, u32[]{:S(2)}) %copy-start.2) | copy-done | bytes 540
  3.6 0.0 copy-start.3
  3.6 0.7 %copy-done.3 = s32[64]{0:T(128)S(1)} copy-done((s32[64]{0:T(128)S(1)}, s32[64]{0:T(128)}, u32[]{:S(2)}) %copy-start.3) | copy-done | bytes 280
  4.3 0.0 copy-start.4
  4.3 0.7 %copy-done.4 = s32[64]{0:T(128)S(1)} copy-done((s32[64]{0:T(128)S(1)}, s32[64]{0:T(128)}, u32[]{:S(2)}) %copy-start.4) | copy-done | bytes 280
  4.9 0.0 copy-start.5
  4.9 0.7 %copy-done.5 = s32[64]{0:T(128)S(1)} copy-done((s32[64]{0:T(128)S(1)}, s32[64]{0:T(128)}, u32[]{:S(2)}) %copy-start.5) | copy-done | bytes 280
  5.6 0.0 copy-start.6
  5.6 0.7 %copy-done.6 = s32[128]{0:T(128)S(1)} copy-done((s32[128]{0:T(128)S(1)}, s32[128]{0:T(128)}, u32[]{:S(2)}) %copy-start.6) | copy-done | bytes 536
  6.2 50.6 %shard_map.95 = (f32[64,8192]{1,0:T(8,128)S(1)}, f32[1,4,256]{2,1,0:T(4,128)S(1)}) custom-call(f32[64,8192]{1,0:T(8,128)S(1)} %copy-done, s32[64,8192]{1,0:T(8,128)} %mask_hbm.1, f32[32,64]{1,0:T(8,128)S(1)} %bitcast.5, f32[129]{0:T(256)S(1)} %copy-done.2, s32[1,64]{1,0:T(1,128)S(1)} %bitcast.6, s32[1,64]{1,0:T(1,128)S(1)} %bitcast.7, s32[1,64]{1,0:T(1,128)S(1)} %bitcast.8, ...), custom_call_target="tpu_custom_call" | custom-call | tf_op jit(solution)/shard_map/pallas_call | solution.py:368
  56.8 1.3 %copy.12 = f32[64,8192]{1,0:T(8,128)} copy(f32[64,8192]{1,0:T(8,128)S(1)} %get-tuple-element.4) | data formatting | bytes 4194304
  58.2 0.6 %copy.13 = f32[1,4,256]{2,1,0:T(4,128)} copy(f32[1,4,256]{2,1,0:T(4,128)S(1)} %get-tuple-element.5) | data formatting | bytes 8192
Async XLA Ops:
  0.6 1.6 %copy-start = (f32[64,8192]{1,0:T(8,128)S(1)}, f32[64,8192]{1,0:T(8,128)}, u32[]{:S(2)}) copy-start(f32[64,8192]{1,0:T(8,128)} %tod_hbm.1) | copy-start | bytes 6291460
  2.2 0.7 %copy-start.1 = (f32[64,32]{0,1:T(8,128)S(1)}, f32[64,32]{0,1:T(8,128)}, u32[]{:S(2)}) copy-start(f32[64,32]{0,1:T(8,128)} %param.10) | copy-start | bytes 24580
  2.9 0.7 %copy-start.2 = (f32[129]{0:T(256)S(1)}, f32[129]{0:T(256)}, u32[]{:S(2)}) copy-start(f32[129]{0:T(256)} %taps_ref.1) | copy-start | bytes 1552
  3.6 0.7 %copy-start.3 = (s32[64]{0:T(128)S(1)}, s32[64]{0:T(128)}, u32[]{:S(2)}) copy-start(s32[64]{0:T(128)} %param.12) | copy-start | bytes 772
  4.3 0.7 %copy-start.4 = (s32[64]{0:T(128)S(1)}, s32[64]{0:T(128)}, u32[]{:S(2)}) copy-start(s32[64]{0:T(128)} %param.13) | copy-start | bytes 772
  4.9 0.7 %copy-start.5 = (s32[64]{0:T(128)S(1)}, s32[64]{0:T(128)}, u32[]{:S(2)}) copy-start(s32[64]{0:T(128)} %param.14) | copy-start | bytes 772
  5.6 0.7 %copy-start.6 = (s32[128]{0:T(128)S(1)}, s32[128]{0:T(128)}, u32[]{:S(2)}) copy-start(s32[128]{0:T(128)} %param.15) | copy-start | bytes 1540

commit v2 on v1

--- a/solution.py
+++ b/solution.py
@@ -39,13 +39,14 @@
 
 
 def kernel(
-    tod_hbm, mask_hbm, coup_ref, taps_ref, cdet_ref, cstart_ref, csrc_ref, owner_ref,
-    filled_ref, templ_ref,
+    tod_hbm, mask_hbm, coup_hbm, taps_hbm, cdet_hbm, cstart_hbm, csrc_hbm, owner_hbm,
+    filled_hbm, templ_ref,
+    coup_ref, taps_ref, cdet_ref, cstart_ref, csrc_ref, owner_ref, filled,
     tod, mask, model, res_hi, res_lo,
     part, acc, got_c, got1, acc1, got2, acc2, got3, amp,
     lhs_p, lhs_m, band,
     slots, dets, first_tile, shift, snip, cnt, cnt_got, tsum, tsum_got,
-    in_sem, c_sem, r_sem, g_sem, gc_sem, t_sem,
+    in_sem, small_sem, out_sem, c_sem, r_sem, g_sem, gc_sem, t_sem,
 ):
     wafer = lax.axis_index("wafer")
     det = lax.axis_index("det")
@@ -74,6 +75,14 @@
 
     def cols(first, width):
         return pl.ds(pl.multiple_of(first, 128), width)
+
+    small = []
+    for k, (src, dst) in enumerate((
+        (coup_hbm, coup_ref), (taps_hbm, taps_ref), (cdet_hbm, cdet_ref),
+        (cstart_hbm, cstart_ref), (csrc_hbm, csrc_ref), (owner_hbm, owner_ref),
+    )):
+        small.append(pltpu.make_async_copy(src, dst, small_sem.at[k]))
+        small[-1].start()
 
     halves = (1 - core, core)
     loads = []
@@ -96,6 +105,7 @@
     for step in range(1, RING):
         pl.semaphore_signal(barrier, inc=1, device_id=along("z", step), device_id_type=MESH)
 
+    small[0].wait()
     coup_t = coup_ref[...]
     c_hi, c_lo = split(coup_t.T)
     lhs_m[...] = jnp.concatenate([c_hi, c_lo, c_hi], axis=1)
@@ -146,6 +156,8 @@
     for s in range(3):
         fill(1, s, acc)
 
+    for one in small[2:]:
+        one.wait()
     owner = 2 * owner_ref[...]
     src_iota = lax.broadcasted_iota(jnp.int32, (128, CROSS), 0)
     of_src = (src_iota == csrc_ref[...]).astype(F32).astype(BF16)
@@ -196,15 +208,10 @@
 
         stage1.append(exchange(r_sem.at[s, 0], axis, src_of, dst_of))
 
-    row = lax.broadcasted_iota(jnp.int32, (256, 128), 0)
-    col = lax.broadcasted_iota(jnp.int32, (256, 128), 1)
-    pos = jnp.where(row < 192, row, row - 256)
-    tap_of = pos - col + 64
-
-    def add_tap(k, total):
-        return total + jnp.where(tap_of == k, taps_ref[k], 0.0)
-
-    b_hi, b_lo = split(lax.fori_loop(0, TAPS, add_tap, jnp.zeros((256, 128), F32)))
+    small[1].wait()
+    line = jnp.concatenate([taps_ref[...], jnp.zeros((1, 256 - TAPS), F32)], axis=1)
+    turned = pltpu.roll(jnp.broadcast_to(line, (128, 256)), 192, 1, stride=1, stride_axis=0)
+    b_hi, b_lo = split(turned.T)
     band[:, 0:128] = b_hi
     band[:, 128:256] = b_lo
 
@@ -332,12 +339,17 @@
         smooth = first[:, 0:128] + (first[:, 128:256] + second)
         for q in range(4):
             span = cols(b * 512 + q * 128, 128)
-            filled_ref[:, span] = jnp.where(
+            filled[:, span] = jnp.where(
                 mask[:, span] != 0, tod[:, span], model[:, span] + smooth[q * ROWS:(q + 1) * ROWS]
             )
         return carry
 
-    lax.fori_loop(0, NS // 512, fill_block, 0)
+    outs = []
+    for part_of in range(4):
+        lax.fori_loop(part_of * 4, part_of * 4 + 4, fill_block, 0)
+        span = pl.ds(part_of * 2048, 2048)
+        outs.append(pltpu.make_async_copy(filled.at[:, span], filled_hbm.at[:, span], out_sem.at[part_of]))
+        outs[-1].start()
 
     def wait_all(src, dst, send, recv):
         every = remote(src.at[0:DET - 1], dst.at[0:DET - 1], send, recv, partner)
@@ -356,6 +368,8 @@
         templ_ref[0, o:o + 1, 0:128] = snip[2 * o:2 * o + 1, :]
         templ_ref[0, o:o + 1, 128:256] = snip[2 * o + 1:2 * o + 2, :]
 
+    for one in outs:
+        one.wait()
     for one in copies_c + copies_a:
         one.wait_send()
     for group in stage1 + stage2 + stage3 + gather2 + gather1:
@@ -364,16 +378,23 @@
 
 
 def on_device(tod, gap_mask, coupling, taps, cross_det, cross_start, cross_src, src_owner):
-    vmem, smem, hbm = (pl.BlockSpec(memory_space=m) for m in (pltpu.VMEM, pltpu.SMEM, pltpu.HBM))
+    vmem, hbm = (pl.BlockSpec(memory_space=m) for m in (pltpu.VMEM, pltpu.HBM))
     return pl.pallas_call(
         kernel,
         out_shape=(
             jax.ShapeDtypeStruct((ROWS, NS), F32),
             jax.ShapeDtypeStruct((1, 4, 256), F32),
         ),
-        in_specs=[hbm, hbm, vmem, smem, vmem, vmem, vmem, vmem],
-        out_specs=(vmem, vmem),
+        in_specs=[hbm] * 8,
+        out_specs=(hbm, vmem),
         scratch_shapes=[
+            pltpu.VMEM((MODES, ROWS), F32),
+            pltpu.VMEM((1, TAPS), F32),
+            pltpu.VMEM((1, CROSS), jnp.int32),
+            pltpu.VMEM((1, CROSS), jnp.int32),
+            pltpu.VMEM((1, CROSS), jnp.int32),
+            pltpu.VMEM((1, 128), jnp.int32),
+            pltpu.VMEM((ROWS, NS), F32),
             pltpu.VMEM((ROWS, NS), F32),
             pltpu.VMEM((ROWS, NS), jnp.int32),
             pltpu.VMEM((ROWS, NS), F32),
@@ -401,6 +422,8 @@
             pltpu.VMEM((DET, 8, 128), F32),
             pltpu.VMEM((DET, 8, 128), F32),
             pltpu.SemaphoreType.DMA((2, 3, 2)),
+            pltpu.SemaphoreType.DMA((6,)),
+            pltpu.SemaphoreType.DMA((4,)),
             pltpu.SemaphoreType.DMA((3, 2)),
             pltpu.SemaphoreType.DMA((3, 3, 3, 2)),
             pltpu.SemaphoreType.DMA((3, 2, 3, 2)),
@@ -408,9 +431,9 @@
             pltpu.SemaphoreType.DMA((4,)),
         ],
         compiler_params=pltpu.CompilerParams(
-            collective_id=0, has_side_effects=True, vmem_limit_bytes=48 << 20
+            collective_id=0, has_side_effects=True, vmem_limit_bytes=67043328
         ),
-    )(tod, gap_mask, coupling.T, taps, *(v.reshape(1, -1) for v in (cross_det, cross_start, cross_src, src_owner)))
+    )(tod, gap_mask, coupling.T, *(v.reshape(1, -1) for v in (taps, cross_det, cross_start, cross_src, src_owner)))
 
 
 def solution(mesh):

time: 59 us -> 55.5 us (0.941)
  local copies, waits for them, and re-layouts: 7.51 us -> 3.66 us
    unnamed x16 -> x4, local copies, waits for them, and re-layouts: 7.51 us -> 3.66 us
where the time goes in v2:
time: 55.5 us; the launch traced here: 55.4 us
  Pallas kernels  51.1 us (92%)
  local copies, waits for them, and re-layouts  3.66 us (7%)
  between operations  0.65 us (1%)
    pallas_call x1, Pallas kernels, on_device(): pl.pallas_call(kernel, out_shape=(jax.ShapeDtypeStruct((ROWS, NS), F32),...  51.1 us
    unnamed x4, local copies, waits for them, and re-layouts  3.66 us

profile of v2, /device:TPU:1, one launch (start us, length us, event | category | flops | bytes accessed | tf_op | source)
XLA Modules:
  0.0 55.4 jit_solution(5884727035141083417)
XLA Ops:
  0.6 51.1 %shard_map.95 = (f32[64,8192]{1,0:T(8,128)}, f32[1,4,256]{2,1,0:T(4,128)}) custom-call(f32[64,8192]{1,0:T(8,128)} %tod_hbm.1, s32[64,8192]{1,0:T(8,128)} %mask_hbm.1, f32[32,64]{1,0:T(8,128)} %bitcast.6, f32[1,129]{1,0:T(1,128)} %bitcast.7, s32[1,64]{1,0:T(1,128)} %bitcast.8, s32[1,64]{1,0:T(1,128)} %bitcast.9, s32[1,64]{1,0:T(1,128)} %bitcast.10, ...), custom_call_target="tpu_custom_call" | custom-call | tf_op jit(solution)/shard_map/pallas_call | solution.py:382
  51.7 0.0 copy-start
  51.7 3.1 %copy.12 = f32[64,8192]{1,0:T(8,128)} copy(f32[64,8192]{1,0:T(8,128)} %get-tuple-element.4) | data formatting | bytes 4194304
  54.8 0.0 copy-done
  54.8 0.6 %copy.13 = f32[1,4,256]{2,1,0:T(4,128)} copy(f32[1,4,256]{2,1,0:T(4,128)S(1)} %copy-done) | data formatting | bytes 8192
Async XLA Ops:
  51.7 3.1 %copy-start = (f32[1,4,256]{2,1,0:T(4,128)S(1)}, f32[1,4,256]{2,1,0:T(4,128)}, u32[]{:S(2)}) copy-start(f32[1,4,256]{2,1,0:T(4,128)} %get-tuple-element.5) | copy-start | bytes 12292

commit v3 on v2

--- a/solution.py
+++ b/solution.py
@@ -43,10 +43,10 @@
     filled_hbm, templ_ref,
     coup_ref, taps_ref, cdet_ref, cstart_ref, csrc_ref, owner_ref, filled,
     tod, mask, model, res_hi, res_lo,
-    part, acc, got_c, got1, acc1, got2, acc2, got3, amp,
+    part, acc, got_c, got_p, acc2, got3, amp,
     lhs_p, lhs_m, band,
     slots, dets, first_tile, shift, snip, cnt, cnt_got, tsum, tsum_got,
-    in_sem, small_sem, out_sem, c_sem, r_sem, g_sem, gc_sem, t_sem,
+    in_sem, small_sem, out_sem, ready_sem, c_sem, p_sem, r_sem, g_sem, gc_sem, t_sem,
 ):
     wafer = lax.axis_index("wafer")
     det = lax.axis_index("det")
@@ -55,15 +55,9 @@
     y = lax.div(det, 2 * RING)
     coord = {"x": x, "y": y, "z": wafer}
 
-    def along(axis, step):
-        xx, yy, zz = x, y, wafer
-        if axis == "x":
-            xx = lax.rem(x + step, RING)
-        elif axis == "y":
-            yy = lax.rem(y + step, RING)
-        else:
-            zz = lax.rem(wafer + step, RING)
-        return (zz, (yy * RING + xx) * 2 + core)
+    def reach(steps):
+        at = {a: lax.rem(coord[a] + steps[a], RING) if steps.get(a) else coord[a] for a in coord}
+        return (at["z"], (at["y"] * RING + at["x"]) * 2 + core)
 
     partner = (wafer, det + 1 - 2 * core)
 
@@ -97,13 +91,10 @@
                 one.start()
             loads.append(pair)
 
+    lines = [reach({a: step}) for a in ("x", "y", "z") for step in range(1, RING)]
     barrier = pltpu.get_barrier_semaphore()
-    for step in range(1, DET):
-        pl.semaphore_signal(
-            barrier, inc=1, device_id=(wafer, lax.rem(det + step, DET)), device_id_type=MESH
-        )
-    for step in range(1, RING):
-        pl.semaphore_signal(barrier, inc=1, device_id=along("z", step), device_id_type=MESH)
+    for to in [partner] + lines:
+        pl.semaphore_signal(barrier, inc=1, device_id=to, device_id_type=MESH)
 
     small[0].wait()
     coup_t = coup_ref[...]
@@ -148,8 +139,10 @@
             remote(part.at[:, :, span], got_c.at[:, :, span], c_sem.at[s, 0], c_sem.at[s, 1], partner)
         )
     fill(0, 0, part)
-    pl.semaphore_wait(barrier, DET - 1 + RING - 1)
+    pl.semaphore_wait(barrier, 1 + len(lines))
     copies_c[0].start()
+    for to in lines:
+        pl.semaphore_signal(ready_sem, inc=1, device_id=to, device_id_type=MESH)
     for s in (1, 2):
         fill(0, s, part)
         copies_c[s].start()
@@ -174,6 +167,49 @@
     first_tile[...] = start >> 7
     shift[...] = start & 127
     cnt[...] = jnp.broadcast_to(jnp.sum(oh_t, axis=1, keepdims=True), (256, 128)).reshape(DET, 8, 128)
+
+    far_first = sorted(
+        ((p, q) for p in range(RING) for q in range(RING) if p or q),
+        key=lambda v: -(min(v[0], RING - v[0]) + min(v[1], RING - v[1])),
+    )
+    pl.semaphore_wait(ready_sem, len(lines))
+    for s, (base, width, order) in enumerate(SETS):
+        copies_c[s].wait_recv()
+        span = pl.ds(base, RING * width)
+        acc[:, :, span] += got_c[:, :, span]
+        for k, (p, q) in enumerate(far_first):
+            block = cols(base + lax.rem(coord[order[0]] + p, RING) * width, width)
+            remote(
+                acc.at[lax.rem(coord[order[1]] + q, RING), :, block], got_p.at[k, :, pl.ds(PLACE[s], width)],
+                p_sem.at[s, 0], p_sem.at[s, 1], reach({order[0]: p, order[1]: q}),
+            ).start()
+
+    small[1].wait()
+    line = jnp.concatenate([taps_ref[...], jnp.zeros((1, 256 - TAPS), F32)], axis=1)
+    turned = pltpu.roll(jnp.broadcast_to(line, (128, 256)), 192, 1, stride=1, stride_axis=0)
+    b_hi, b_lo = split(turned.T)
+    band[:, 0:128] = b_hi
+    band[:, 128:256] = b_lo
+
+    def from_plane(s, rows, sems):
+        every = got_p.at[:, 0:rows, pl.ds(PLACE[s], SETS[s][1])]
+        return remote(every, every, sems.at[s, 0], sems.at[s, 1], partner)
+
+    axis3 = []
+    for s, (base, width, order) in enumerate(SETS):
+        from_plane(s, 16, p_sem).wait_recv()
+        span = pl.ds(PLACE[s], width)
+        total = acc[coord[order[1]], :, cols(base + coord[order[0]] * width, width)]
+        for k in range(len(far_first)):
+            total += got_p[k, :, span]
+        acc2[:, span] = total
+        for step in range(1, RING):
+            axis3.append(remote(
+                acc2.at[:, span], got3.at[step - 1, :, span],
+                r_sem.at[s, step - 1, 0], r_sem.at[s, step - 1, 1], reach({order[2]: step}),
+            ))
+            axis3[-1].start()
+
     copies_n = []
     for step in range(1, DET):
         to = lax.rem(det + step, DET)
@@ -182,105 +218,16 @@
         )
         copies_n[-1].start()
 
-    def exchange(sem, axis, src_of, dst_of):
-        made = []
-        for step in range(1, RING):
-            made.append(
-                remote(src_of(step), dst_of(step), sem.at[step - 1, 0], sem.at[step - 1, 1], along(axis, step))
-            )
-        for one in made:
-            one.start()
-        return made
-
-    stage1 = []
     for s, (base, width, order) in enumerate(SETS):
-        copies_c[s].wait_recv()
-        span = pl.ds(base, RING * width)
-        acc[:, :, span] += got_c[:, :, span]
-        axis = order[0]
-
-        def src_of(step, base=base, width=width, axis=axis):
-            to = lax.rem(coord[axis] + step, RING)
-            return acc.at[:, :, cols(base + to * width, width)]
-
-        def dst_of(step, s=s, width=width):
-            return got1.at[step - 1, :, :, pl.ds(PLACE[s], width)]
-
-        stage1.append(exchange(r_sem.at[s, 0], axis, src_of, dst_of))
-
-    small[1].wait()
-    line = jnp.concatenate([taps_ref[...], jnp.zeros((1, 256 - TAPS), F32)], axis=1)
-    turned = pltpu.roll(jnp.broadcast_to(line, (128, 256)), 192, 1, stride=1, stride_axis=0)
-    b_hi, b_lo = split(turned.T)
-    band[:, 0:128] = b_hi
-    band[:, 128:256] = b_lo
-
-    stage2 = []
-    for s, (base, width, order) in enumerate(SETS):
-        for one in stage1[s]:
-            one.wait_recv()
-        mine = cols(base + coord[order[0]] * width, width)
-        span = pl.ds(PLACE[s], width)
-        acc1[:, :, span] = (acc[:, :, mine] + got1[0, :, :, span]) + (got1[1, :, :, span] + got1[2, :, :, span])
-        axis = order[1]
-
-        def src_of(step, span=span, axis=axis):
-            return acc1.at[lax.rem(coord[axis] + step, RING), :, span]
-
-        def dst_of(step, span=span):
-            return got2.at[step - 1, :, span]
-
-        stage2.append(exchange(r_sem.at[s, 1], axis, src_of, dst_of))
-
-    stage3 = []
-    for s, (base, width, order) in enumerate(SETS):
-        for one in stage2[s]:
-            one.wait_recv()
-        span = pl.ds(PLACE[s], width)
-        acc2[:, span] = (acc1[coord[order[1]], :, span] + got2[0, :, span]) + (got2[1, :, span] + got2[2, :, span])
-
-        def src_of(step, span=span):
-            return acc2.at[:, span]
-
-        def dst_of(step, span=span):
-            return got3.at[step - 1, :, span]
-
-        stage3.append(exchange(r_sem.at[s, 2], order[2], src_of, dst_of))
-
-    gather2 = []
-    for s, (base, width, order) in enumerate(SETS):
-        for one in stage3[s]:
+        for one in axis3[3 * s:3 * s + 3]:
             one.wait_recv()
         span = pl.ds(PLACE[s], width)
         whole = (acc2[:, span] + got3[0, :, span]) + (got3[1, :, span] + got3[2, :, span])
         block = cols(core * HALF + base + coord[order[0]] * width, width)
         amp[coord[order[1]], :, block] = whole[0:8] / (whole[8:16] + 1.0)
-
-        def here(step, block=block, j=coord[order[1]]):
-            return amp.at[j, :, block]
-
-        gather2.append(exchange(g_sem.at[s, 0], order[1], here, here))
-
-    gather1 = []
-    for s, (base, width, order) in enumerate(SETS):
-        for one in gather2[s]:
-            one.wait_recv()
-        block = cols(core * HALF + base + coord[order[0]] * width, width)
-
-        def here(step, block=block):
-            return amp.at[:, :, block]
-
-        gather1.append(exchange(g_sem.at[s, 1], order[0], here, here))
-
-    copies_a = []
-    for s, (base, width, order) in enumerate(SETS):
-        for one in gather1[s]:
-            one.wait_recv()
-        span = cols(core * HALF + base, RING * width)
-        copies_a.append(remote(amp.at[:, :, span], amp.at[:, :, span], gc_sem.at[s, 0], gc_sem.at[s, 1], partner))
-        copies_a[-1].start()
-    for one in copies_a:
-        one.wait_recv()
+        here = amp.at[coord[order[1]], :, block]
+        for p, q in far_first:
+            remote(here, here, g_sem.at[s, 0], g_sem.at[s, 1], reach({order[0]: p, order[1]: q})).start()
 
     for edge in (res_hi, res_lo):
         edge[:, 0:128] = jnp.zeros((ROWS, 128), BF16)
@@ -302,7 +249,19 @@
                 wide[w] = jnp.where(tile == b * 4 + q - w, lines[:, 128 * q:128 * q + 128], wide[w])
         return tuple(wide)
 
-    wide = lax.fori_loop(0, NS // 512, model_block, (jnp.zeros((CROSS, 128), F32),) * 3)
+    wide = (jnp.zeros((CROSS, 128), F32),) * 3
+    copies_a = []
+    for s, (base, width, _) in enumerate(SETS):
+        from_plane(s, 8, g_sem).wait_recv()
+        half = amp.at[:, :, cols(core * HALF + base, RING * width)]
+        copies_a.append(remote(half, half, gc_sem.at[s, 0], gc_sem.at[s, 1], partner))
+        copies_a[-1].start()
+        first = core * (HALF // 512) + base // 512
+        wide = lax.fori_loop(first, first + RING * width // 512, model_block, wide)
+    for s, (base, width, _) in enumerate(SETS):
+        copies_a[s].wait_recv()
+        first = (1 - core) * (HALF // 512) + base // 512
+        wide = lax.fori_loop(first, first + RING * width // 512, model_block, wide)
 
     rows = jnp.concatenate(wide, axis=1)
     rest = jnp.concatenate([shift[...]] * 3, axis=1)
@@ -370,11 +329,11 @@
 
     for one in outs:
         one.wait()
-    for one in copies_c + copies_a:
+    for one in copies_c + copies_a + axis3:
         one.wait_send()
-    for group in stage1 + stage2 + stage3 + gather2 + gather1:
-        for one in group:
-            one.wait_send()
+    for s in range(3):
+        from_plane(s, 16, p_sem).wait_send()
+        from_plane(s, 8, g_sem).wait_send()
 
 
 def on_device(tod, gap_mask, coupling, taps, cross_det, cross_start, cross_src, src_owner):
@@ -403,9 +362,7 @@
             pltpu.VMEM((RING, 16, HALF), F32),
             pltpu.VMEM((RING, 16, HALF), F32),
             pltpu.VMEM((RING, 16, HALF), F32),
-            pltpu.VMEM((3, RING, 16, BLOCKS), F32),
-            pltpu.VMEM((RING, 16, BLOCKS), F32),
-            pltpu.VMEM((3, 16, BLOCKS), F32),
+            pltpu.VMEM((RING * RING - 1, 16, BLOCKS), F32),
             pltpu.VMEM((16, BLOCKS), F32),
             pltpu.VMEM((3, 16, BLOCKS), F32),
             pltpu.VMEM((RING, 8, NS), F32),
@@ -424,9 +381,11 @@
             pltpu.SemaphoreType.DMA((2, 3, 2)),
             pltpu.SemaphoreType.DMA((6,)),
             pltpu.SemaphoreType.DMA((4,)),
+            pltpu.SemaphoreType.REGULAR,
             pltpu.SemaphoreType.DMA((3, 2)),
-            pltpu.SemaphoreType.DMA((3, 3, 3, 2)),
-            pltpu.SemaphoreType.DMA((3, 2, 3, 2)),
+            pltpu.SemaphoreType.DMA((3, 2)),
+            pltpu.SemaphoreType.DMA((3, 3, 2)),
+            pltpu.SemaphoreType.DMA((3, 2)),
             pltpu.SemaphoreType.DMA((3, 2)),
             pltpu.SemaphoreType.DMA((4,)),
         ],

time: 55.5 us -> 48.1 us (0.87)
  Pallas kernels: 51.1 us -> 43.6 us
    pallas_call x1, Pallas kernels: 51.1 us -> 43.6 us  [on_device(): pl.pallas_call(kernel, out_shape=(jax.ShapeDtypeStruct((ROWS, NS), F32),...]
where the time goes in v3:
time: 48.1 us; the launch traced here: 48 us
  Pallas kernels  43.6 us (91%)
  local copies, waits for them, and re-layouts  3.66 us (8%)
  between operations  0.65 us (1%)
    pallas_call x1, Pallas kernels, on_device(): pl.pallas_call(kernel, out_shape=(jax.ShapeDtypeStruct((ROWS, NS), F32),...  43.6 us
    unnamed x4, local copies, waits for them, and re-layouts  3.66 us

profile of v3, /device:TPU:1, one launch (start us, length us, event | category | flops | bytes accessed | tf_op | source)
XLA Modules:
  0.0 48.0 jit_solution(5173897621499092142)
XLA Ops:
  0.6 43.6 %shard_map.95 = (f32[64,8192]{1,0:T(8,128)}, f32[1,4,256]{2,1,0:T(4,128)}) custom-call(f32[64,8192]{1,0:T(8,128)} %tod_hbm.1, s32[64,8192]{1,0:T(8,128)} %mask_hbm.1, f32[32,64]{1,0:T(8,128)} %bitcast.6, f32[1,129]{1,0:T(1,128)} %bitcast.7, s32[1,64]{1,0:T(1,128)} %bitcast.8, s32[1,64]{1,0:T(1,128)} %bitcast.9, s32[1,64]{1,0:T(1,128)} %bitcast.10, ...), custom_call_target="tpu_custom_call" | custom-call | tf_op jit(solution)/shard_map/pallas_call | solution.py:341
  44.3 0.0 copy-start
  44.3 3.1 %copy.12 = f32[64,8192]{1,0:T(8,128)} copy(f32[64,8192]{1,0:T(8,128)} %get-tuple-element.4) | data formatting | bytes 4194304
  47.4 0.0 copy-done
  47.4 0.6 %copy.13 = f32[1,4,256]{2,1,0:T(4,128)} copy(f32[1,4,256]{2,1,0:T(4,128)S(1)} %copy-done) | data formatting | bytes 8192
Async XLA Ops:
  44.3 3.1 %copy-start = (f32[1,4,256]{2,1,0:T(4,128)S(1)}, f32[1,4,256]{2,1,0:T(4,128)}, u32[]{:S(2)}) copy-start(f32[1,4,256]{2,1,0:T(4,128)} %get-tuple-element.5) | copy-start | bytes 12292

commit v4 on v3

--- a/solution.py
+++ b/solution.py
@@ -40,13 +40,13 @@
 
 def kernel(
     tod_hbm, mask_hbm, coup_hbm, taps_hbm, cdet_hbm, cstart_hbm, csrc_hbm, owner_hbm,
-    filled_hbm, templ_ref,
-    coup_ref, taps_ref, cdet_ref, cstart_ref, csrc_ref, owner_ref, filled,
+    filled, templ_ref,
+    coup_ref, taps_ref, cdet_ref, cstart_ref, csrc_ref, owner_ref,
     tod, mask, model, res_hi, res_lo,
     part, acc, got_c, got_p, acc2, got3, amp,
     lhs_p, lhs_m, band,
-    slots, dets, first_tile, shift, snip, cnt, cnt_got, tsum, tsum_got,
-    in_sem, small_sem, out_sem, ready_sem, c_sem, p_sem, r_sem, g_sem, gc_sem, t_sem,
+    slots, dets, first_tile, shift, tod_snip, good_snip, snip, cnt, cnt_got, tsum, tsum_got,
+    in_sem, small_sem, ready_sem, c_sem, p_sem, r_sem, g_sem, gc_sem, t_sem,
 ):
     wafer = lax.axis_index("wafer")
     det = lax.axis_index("det")
@@ -99,7 +99,7 @@
     small[0].wait()
     coup_t = coup_ref[...]
     c_hi, c_lo = split(coup_t.T)
-    lhs_m[...] = jnp.concatenate([c_hi, c_lo, c_hi], axis=1)
+    lhs_m[0:ROWS, :] = jnp.concatenate([c_hi, c_lo, c_hi], axis=1)
     t_hi, t_lo = split(coup_t)
     w_hi, w_lo = split(coup_t * coup_t)
     zero = jnp.zeros((MODES, ROWS), BF16)
@@ -138,16 +138,42 @@
         copies_c.append(
             remote(part.at[:, :, span], got_c.at[:, :, span], c_sem.at[s, 0], c_sem.at[s, 1], partner)
         )
-    fill(0, 0, part)
+    for s in range(3):
+        fill(0, s, part)
     pl.semaphore_wait(barrier, 1 + len(lines))
-    copies_c[0].start()
+    for one in copies_c:
+        one.start()
     for to in lines:
         pl.semaphore_signal(ready_sem, inc=1, device_id=to, device_id_type=MESH)
-    for s in (1, 2):
-        fill(0, s, part)
-        copies_c[s].start()
-    for s in range(3):
+
+    steps = sorted(
+        ((p, q) for p in range(RING) for q in range(RING) if p or q),
+        key=lambda v: -(min(v[0], RING - v[0]) + min(v[1], RING - v[1])),
+    )
+    on_line = [v for v in steps if not (v[0] and v[1])]
+    off_line = [v for v in steps if v[0] and v[1]]
+
+    def scatter(s, which):
+        base, width, order = SETS[s]
+        for p, q in which:
+            block = cols(base + lax.rem(coord[order[0]] + p, RING) * width, width)
+            remote(
+                acc.at[lax.rem(coord[order[1]] + q, RING), :, block],
+                got_p.at[steps.index((p, q)), :, pl.ds(PLACE[s], width)],
+                p_sem.at[s, 0], p_sem.at[s, 1], reach({order[0]: p, order[1]: q}),
+            ).start()
+
+    for s, (base, width, order) in enumerate(SETS):
         fill(1, s, acc)
+        copies_c[s].wait_recv()
+        span = pl.ds(base, RING * width)
+        acc[:, :, span] += got_c[:, :, span]
+        if s == 0:
+            scatter(s, on_line)
+            pl.semaphore_wait(ready_sem, len(lines))
+            scatter(s, off_line)
+        else:
+            scatter(s, steps)
 
     for one in small[2:]:
         one.wait()
@@ -166,23 +192,8 @@
     start = jnp.broadcast_to(cstart_ref[...], (128, CROSS)).T
     first_tile[...] = start >> 7
     shift[...] = start & 127
+    lhs_m[ROWS:ROWS + CROSS, :] = dot(of_det, lhs_m[0:ROWS, :]).astype(BF16)
     cnt[...] = jnp.broadcast_to(jnp.sum(oh_t, axis=1, keepdims=True), (256, 128)).reshape(DET, 8, 128)
-
-    far_first = sorted(
-        ((p, q) for p in range(RING) for q in range(RING) if p or q),
-        key=lambda v: -(min(v[0], RING - v[0]) + min(v[1], RING - v[1])),
-    )
-    pl.semaphore_wait(ready_sem, len(lines))
-    for s, (base, width, order) in enumerate(SETS):
-        copies_c[s].wait_recv()
-        span = pl.ds(base, RING * width)
-        acc[:, :, span] += got_c[:, :, span]
-        for k, (p, q) in enumerate(far_first):
-            block = cols(base + lax.rem(coord[order[0]] + p, RING) * width, width)
-            remote(
-                acc.at[lax.rem(coord[order[1]] + q, RING), :, block], got_p.at[k, :, pl.ds(PLACE[s], width)],
-                p_sem.at[s, 0], p_sem.at[s, 1], reach({order[0]: p, order[1]: q}),
-            ).start()
 
     small[1].wait()
     line = jnp.concatenate([taps_ref[...], jnp.zeros((1, 256 - TAPS), F32)], axis=1)
@@ -191,6 +202,40 @@
     band[:, 0:128] = b_hi
     band[:, 128:256] = b_lo
 
+    def choose(b, lines, wide):
+        tile = first_tile[...]
+        at = {v: tile == b * 4 + v for v in range(-2, 4)}
+        wide = list(wide)
+        for q in range(4):
+            for w in range(3):
+                wide[w] = jnp.where(at[q - w], lines[:, 128 * q:128 * q + 128], wide[w])
+        return tuple(wide)
+
+    def shifted(wide):
+        rows = jnp.concatenate(wide, axis=1)
+        rest = jnp.concatenate([shift[...]] * 3, axis=1)
+        for bit in range(7):
+            moved = pltpu.roll(rows, 384 - (1 << bit), 1)
+            rows = jnp.where((rest & (1 << bit)) != 0, moved, rows)
+        return rows[:, 0:256]
+
+    no_tiles = (jnp.zeros((CROSS, 128), F32),) * 3
+
+    def tod_block(b, wide):
+        span = cols(b * 512, 512)
+        v_hi, v_lo = split(jnp.where(mask[:, span] != 0, tod[:, span], 0.0))
+        return choose(b, dot(dets[...], jnp.concatenate([v_hi, v_lo], axis=0)), wide)
+
+    def good_block(b, wide):
+        g = mask[:, cols(b * 512, 512)].astype(F32).astype(BF16)
+        return choose(b, dot(dets[:, 0:ROWS], g), wide)
+
+    tod_snip[...] = shifted(lax.fori_loop(0, NS // 512, tod_block, no_tiles))
+    good_snip[...] = shifted(lax.fori_loop(0, NS // 512, good_block, no_tiles))
+    for edge in (res_hi, res_lo):
+        edge[:, 0:128] = jnp.zeros((ROWS, 128), BF16)
+        edge[:, 128 + NS:256 + NS] = jnp.zeros((ROWS, 128), BF16)
+
     def from_plane(s, rows, sems):
         every = got_p.at[:, 0:rows, pl.ds(PLACE[s], SETS[s][1])]
         return remote(every, every, sems.at[s, 0], sems.at[s, 1], partner)
@@ -200,7 +245,7 @@
         from_plane(s, 16, p_sem).wait_recv()
         span = pl.ds(PLACE[s], width)
         total = acc[coord[order[1]], :, cols(base + coord[order[0]] * width, width)]
-        for k in range(len(far_first)):
+        for k in range(len(steps)):
             total += got_p[k, :, span]
         acc2[:, span] = total
         for step in range(1, RING):
@@ -226,30 +271,17 @@
         block = cols(core * HALF + base + coord[order[0]] * width, width)
         amp[coord[order[1]], :, block] = whole[0:8] / (whole[8:16] + 1.0)
         here = amp.at[coord[order[1]], :, block]
-        for p, q in far_first:
+        for p, q in steps:
             remote(here, here, g_sem.at[s, 0], g_sem.at[s, 1], reach({order[0]: p, order[1]: q})).start()
-
-    for edge in (res_hi, res_lo):
-        edge[:, 0:128] = jnp.zeros((ROWS, 128), BF16)
-        edge[:, 128 + NS:256 + NS] = jnp.zeros((ROWS, 128), BF16)
 
     def model_block(b, wide):
         span = cols(b * 512, 512)
         a_hi, a_lo = split(amp[:, :, span].reshape(MODES, 512))
         value = dot(lhs_m[...], jnp.concatenate([a_hi, a_hi, a_lo], axis=0))
-        model[:, span] = value
-        r_hi, r_lo = split(jnp.where(mask[:, span] != 0, tod[:, span] - value, 0.0))
-        res_hi[:, cols(b * 512 + 128, 512)] = r_hi
-        res_lo[:, cols(b * 512 + 128, 512)] = r_lo
-        lines = dot(dets[...], jnp.concatenate([r_hi, r_lo], axis=0))
-        tile = first_tile[...]
-        wide = list(wide)
-        for q in range(4):
-            for w in range(3):
-                wide[w] = jnp.where(tile == b * 4 + q - w, lines[:, 128 * q:128 * q + 128], wide[w])
-        return tuple(wide)
-
-    wide = (jnp.zeros((CROSS, 128), F32),) * 3
+        model[:, span] = value[0:ROWS]
+        return choose(b, value[ROWS:ROWS + CROSS], wide)
+
+    wide = no_tiles
     copies_a = []
     for s, (base, width, _) in enumerate(SETS):
         from_plane(s, 8, g_sem).wait_recv()
@@ -263,11 +295,7 @@
         first = (1 - core) * (HALF // 512) + base // 512
         wide = lax.fori_loop(first, first + RING * width // 512, model_block, wide)
 
-    rows = jnp.concatenate(wide, axis=1)
-    rest = jnp.concatenate([shift[...]] * 3, axis=1)
-    for bit in range(7):
-        moved = pltpu.roll(rows, 384 - (1 << bit), 1)
-        rows = jnp.where((rest & (1 << bit)) != 0, moved, rows)
+    rows = jnp.where(good_snip[...] != 0.0, tod_snip[...] - shifted(wide), 0.0)
     snip[0:CROSS, :] = rows[:, 0:128]
     snip[CROSS:2 * CROSS, :] = rows[:, 128:256]
     s_hi, s_lo = split(snip[...])
@@ -280,6 +308,14 @@
         )
         copies_t[-1].start()
 
+    def resid_block(b, carry):
+        span = cols(b * 512, 512)
+        r_hi, r_lo = split(jnp.where(mask[:, span] != 0, tod[:, span] - model[:, span], 0.0))
+        res_hi[:, cols(b * 512 + 128, 512)] = r_hi
+        res_lo[:, cols(b * 512 + 128, 512)] = r_lo
+        return carry
+
+    lax.fori_loop(0, NS // 512, resid_block, 0)
     lane64 = lax.broadcasted_iota(jnp.int32, (ROWS, 128), 1) < 64
 
     def fill_block(b, carry):
@@ -303,12 +339,7 @@
             )
         return carry
 
-    outs = []
-    for part_of in range(4):
-        lax.fori_loop(part_of * 4, part_of * 4 + 4, fill_block, 0)
-        span = pl.ds(part_of * 2048, 2048)
-        outs.append(pltpu.make_async_copy(filled.at[:, span], filled_hbm.at[:, span], out_sem.at[part_of]))
-        outs[-1].start()
+    lax.fori_loop(0, NS // 512, fill_block, 0)
 
     def wait_all(src, dst, send, recv):
         every = remote(src.at[0:DET - 1], dst.at[0:DET - 1], send, recv, partner)
@@ -327,8 +358,6 @@
         templ_ref[0, o:o + 1, 0:128] = snip[2 * o:2 * o + 1, :]
         templ_ref[0, o:o + 1, 128:256] = snip[2 * o + 1:2 * o + 2, :]
 
-    for one in outs:
-        one.wait()
     for one in copies_c + copies_a + axis3:
         one.wait_send()
     for s in range(3):
@@ -336,16 +365,25 @@
         from_plane(s, 8, g_sem).wait_send()
 
 
+def hand_out(filled, templ, filled_out, templ_out, sem):
+    copies = [
+        pltpu.make_async_copy(filled, filled_out, sem.at[0]),
+        pltpu.make_async_copy(templ, templ_out, sem.at[1]),
+    ]
+    for one in copies:
+        one.start()
+    for one in copies:
+        one.wait()
+
+
 def on_device(tod, gap_mask, coupling, taps, cross_det, cross_start, cross_src, src_owner):
     vmem, hbm = (pl.BlockSpec(memory_space=m) for m in (pltpu.VMEM, pltpu.HBM))
-    return pl.pallas_call(
+    shapes = (jax.ShapeDtypeStruct((ROWS, NS), F32), jax.ShapeDtypeStruct((1, 4, 256), F32))
+    results = pl.pallas_call(
         kernel,
-        out_shape=(
-            jax.ShapeDtypeStruct((ROWS, NS), F32),
-            jax.ShapeDtypeStruct((1, 4, 256), F32),
-        ),
+        out_shape=shapes,
         in_specs=[hbm] * 8,
-        out_specs=(hbm, vmem),
+        out_specs=(vmem, vmem),
         scratch_shapes=[
             pltpu.VMEM((MODES, ROWS), F32),
             pltpu.VMEM((1, TAPS), F32),
@@ -353,7 +391,6 @@
             pltpu.VMEM((1, CROSS), jnp.int32),
             pltpu.VMEM((1, CROSS), jnp.int32),
             pltpu.VMEM((1, 128), jnp.int32),
-            pltpu.VMEM((ROWS, NS), F32),
             pltpu.VMEM((ROWS, NS), F32),
             pltpu.VMEM((ROWS, NS), jnp.int32),
             pltpu.VMEM((ROWS, NS), F32),
@@ -367,12 +404,14 @@
             pltpu.VMEM((3, 16, BLOCKS), F32),
             pltpu.VMEM((RING, 8, NS), F32),
             pltpu.VMEM((96, 256), BF16),
-            pltpu.VMEM((ROWS, 96), BF16),
+            pltpu.VMEM((ROWS + CROSS, 96), BF16),
             pltpu.VMEM((256, 256), BF16),
             pltpu.VMEM((256, 256), BF16),
             pltpu.VMEM((CROSS, 128), BF16),
             pltpu.VMEM((CROSS, 128), jnp.int32),
             pltpu.VMEM((CROSS, 128), jnp.int32),
+            pltpu.VMEM((CROSS, 256), F32),
+            pltpu.VMEM((CROSS, 256), F32),
             pltpu.VMEM((2 * CROSS, 128), F32),
             pltpu.VMEM((DET, 8, 128), F32),
             pltpu.VMEM((DET, 8, 128), F32),
@@ -380,7 +419,6 @@
             pltpu.VMEM((DET, 8, 128), F32),
             pltpu.SemaphoreType.DMA((2, 3, 2)),
             pltpu.SemaphoreType.DMA((6,)),
-            pltpu.SemaphoreType.DMA((4,)),
             pltpu.SemaphoreType.REGULAR,
             pltpu.SemaphoreType.DMA((3, 2)),
             pltpu.SemaphoreType.DMA((3, 2)),
@@ -390,9 +428,18 @@
             pltpu.SemaphoreType.DMA((4,)),
         ],
         compiler_params=pltpu.CompilerParams(
-            collective_id=0, has_side_effects=True, vmem_limit_bytes=67043328
+            collective_id=0, has_side_effects=True, vmem_limit_bytes=40 << 20
         ),
-    )(tod, gap_mask, coupling.T, *(v.reshape(1, -1) for v in (taps, cross_det, cross_start, cross_src, src_owner)))
+    )(*(pltpu.with_memory_space_constraint(v, pltpu.HBM) for v in (tod, gap_mask, coupling.T, *(v.reshape(1, -1) for v in (taps, cross_det, cross_start, cross_src, src_owner)))))
+
+    return pl.pallas_call(
+        hand_out,
+        out_shape=shapes,
+        in_specs=[vmem] * 2,
+        out_specs=(hbm, hbm),
+        scratch_shapes=[pltpu.SemaphoreType.DMA((2,))],
+        compiler_params=pltpu.CompilerParams(vmem_limit_bytes=1 << 20),
+    )(*results)
 
 
 def solution(mesh):

time: 48.1 us -> 42.5 us (0.88)
  local copies, waits for them, and re-layouts: 3.66 us -> 0 us
  Pallas kernels: 43.6 us -> 41.7 us
    unnamed x4 -> x0, local copies, waits for them, and re-layouts: 3.66 us -> none
    pallas_call x1 -> x2, Pallas kernels: 43.6 us -> 41.7 us  [the longest x1 40.4 us: on_device(): pl.pallas_call(kernel, out_shape=shapes, in_specs=[hbm] * 8, out_specs=(v...]
where the time goes in v4:
time: 42.5 us; the launch traced here: 42.4 us
  Pallas kernels  41.7 us (98%)
  between operations  0.64 us (2%)
    pallas_call x1, Pallas kernels, on_device(): pl.pallas_call(kernel, out_shape=shapes, in_specs=[hbm] * 8, out_specs=(v...  40.4 us
    pallas_call x1, Pallas kernels, on_device(): pl.pallas_call(hand_out, out_shape=shapes, in_specs=[vmem] * 2, out_specs...  1.34 us

profile of v4, /device:TPU:1, one launch (start us, length us, event | category | flops | bytes accessed | tf_op | source)
XLA Modules:
  0.0 42.4 jit_solution(15178616707971075462)
XLA Ops:
  0.6 40.4 %shard_map.95 = (f32[64,8192]{1,0:T(8,128)S(1)}, f32[1,4,256]{2,1,0:T(4,128)S(1)}) custom-call(f32[64,8192]{1,0:T(8,128)} %tod_hbm.1, s32[64,8192]{1,0:T(8,128)} %mask_hbm.1, f32[32,64]{1,0:T(8,128)} %bitcast.6, f32[1,129]{1,0:T(1,128)} %bitcast.7, s32[1,64]{1,0:T(1,128)} %bitcast.8, s32[1,64]{1,0:T(1,128)} %bitcast.9, s32[1,64]{1,0:T(1,128)} %bitcast.10, ...), custom_call_target="tpu_custom_call" | custom-call | tf_op jit(solution)/shard_map/pallas_call | solution.py:382
  41.0 1.3 %shard_map.96 = (f32[64,8192]{1,0:T(8,128)}, f32[1,4,256]{2,1,0:T(4,128)}) custom-call(f32[64,8192]{1,0:T(8,128)S(1)} %get-tuple-element.4.filled, f32[1,4,256]{2,1,0:T(4,128)S(1)} %get-tuple-element.5.templ), custom_call_target="tpu_custom_call" | custom-call | tf_op jit(solution)/shard_map/pallas_call | solution.py:435

commit v5 on v4

--- a/solution.py
+++ b/solution.py
@@ -20,11 +20,17 @@
 RING = 4
 DET = 32
 SETS = (
-    (0, 384, ("x", "y", "z")),
-    (1536, 384, ("y", "z", "x")),
-    (3072, 256, ("z", "x", "y")),
+    (0, 256, ("x", "y", "z")),
+    (1024, 128, ("y", "z", "x")),
+    (1536, 128, ("z", "x", "y")),
+    (2048, 128, ("x", "y", "z")),
+    (2560, 256, ("y", "z", "x")),
+    (3584, 128, ("z", "x", "y")),
 )
-PLACE = (0, 384, 768)
+GROUPS = ((0, 1, 2), (3, 4, 5))
+WIDE = HALF // len(GROUPS)
+CHUNK = 512
+PLACE = (0, 256, 384, 512, 640, 896)
 BLOCKS = 1024
 
 
@@ -79,17 +85,16 @@
         small[-1].start()
 
     halves = (1 - core, core)
-    loads = []
+    loads = {}
     for h in range(2):
-        for s, (base, width, _) in enumerate(SETS):
-            span = cols(halves[h] * HALF + base, RING * width)
-            pair = (
-                pltpu.make_async_copy(tod_hbm.at[:, span], tod.at[:, span], in_sem.at[h, s, 0]),
-                pltpu.make_async_copy(mask_hbm.at[:, span], mask.at[:, span], in_sem.at[h, s, 1]),
+        for g in range(len(GROUPS)):
+            span = cols(halves[h] * HALF + g * WIDE, WIDE)
+            loads[h, g] = (
+                pltpu.make_async_copy(tod_hbm.at[:, span], tod.at[:, span], in_sem.at[h, g, 0]),
+                pltpu.make_async_copy(mask_hbm.at[:, span], mask.at[:, span], in_sem.at[h, g, 1]),
             )
-            for one in pair:
+            for one in loads[h, g]:
                 one.start()
-            loads.append(pair)
 
     lines = [reach({a: step}) for a in ("x", "y", "z") for step in range(1, RING)]
     barrier = pltpu.get_barrier_semaphore()
@@ -116,35 +121,35 @@
         out = dot(lhs_p[...], jnp.concatenate([v_hi, v_hi, v_lo, g], axis=0))
         return out[0:32], out[32:64] + out[64:96]
 
-    def fill(h, s, dst):
-        base, width, _ = SETS[s]
-        for one in loads[h * 3 + s]:
+    def fill(h, g, dst):
+        for one in loads[h, g]:
             one.wait()
 
         def body(i, carry):
-            local = base + i * width
-            sums, weights = partial_sums(halves[h] * HALF + local, width)
-            span = cols(local, width)
+            local = g * WIDE + i * CHUNK
+            sums, weights = partial_sums(halves[h] * HALF + local, CHUNK)
+            span = cols(local, CHUNK)
             for j in range(RING):
                 dst[j, 0:8, span] = sums[8 * j:8 * j + 8]
                 dst[j, 8:16, span] = weights[8 * j:8 * j + 8]
             return carry
 
-        lax.fori_loop(0, RING, body, 0)
+        lax.fori_loop(0, WIDE // CHUNK, body, 0)
 
     copies_c = []
-    for s, (base, width, _) in enumerate(SETS):
-        span = pl.ds(base, RING * width)
+    for g in range(len(GROUPS)):
+        span = pl.ds(g * WIDE, WIDE)
         copies_c.append(
-            remote(part.at[:, :, span], got_c.at[:, :, span], c_sem.at[s, 0], c_sem.at[s, 1], partner)
+            remote(part.at[:, :, span], got_c.at[:, :, span], c_sem.at[g, 0], c_sem.at[g, 1], partner)
         )
-    for s in range(3):
-        fill(0, s, part)
+    fill(0, 0, part)
+    fill(0, 1, part)
     pl.semaphore_wait(barrier, 1 + len(lines))
-    for one in copies_c:
-        one.start()
+    copies_c[0].start()
     for to in lines:
         pl.semaphore_signal(ready_sem, inc=1, device_id=to, device_id_type=MESH)
+    fill(1, 0, acc)
+    copies_c[1].start()
 
     steps = sorted(
         ((p, q) for p in range(RING) for q in range(RING) if p or q),
@@ -163,17 +168,21 @@
                 p_sem.at[s, 0], p_sem.at[s, 1], reach({order[0]: p, order[1]: q}),
             ).start()
 
-    for s, (base, width, order) in enumerate(SETS):
-        fill(1, s, acc)
-        copies_c[s].wait_recv()
-        span = pl.ds(base, RING * width)
+    def take(g):
+        copies_c[g].wait_recv()
+        span = pl.ds(g * WIDE, WIDE)
         acc[:, :, span] += got_c[:, :, span]
-        if s == 0:
-            scatter(s, on_line)
-            pl.semaphore_wait(ready_sem, len(lines))
-            scatter(s, off_line)
-        else:
-            scatter(s, steps)
+
+    take(0)
+    for s in GROUPS[0]:
+        scatter(s, on_line)
+    pl.semaphore_wait(ready_sem, len(lines))
+    for s in GROUPS[0]:
+        scatter(s, off_line)
+    fill(1, 1, acc)
+    take(1)
+    for s in GROUPS[1]:
+        scatter(s, steps)
 
     for one in small[2:]:
         one.wait()
@@ -231,7 +240,6 @@
         return choose(b, dot(dets[:, 0:ROWS], g), wide)
 
     tod_snip[...] = shifted(lax.fori_loop(0, NS // 512, tod_block, no_tiles))
-    good_snip[...] = shifted(lax.fori_loop(0, NS // 512, good_block, no_tiles))
     for edge in (res_hi, res_lo):
         edge[:, 0:128] = jnp.zeros((ROWS, 128), BF16)
         edge[:, 128 + NS:256 + NS] = jnp.zeros((ROWS, 128), BF16)
@@ -242,6 +250,8 @@
 
     axis3 = []
     for s, (base, width, order) in enumerate(SETS):
+        if s == GROUPS[1][0]:
+            good_snip[...] = shifted(lax.fori_loop(0, NS // 512, good_block, no_tiles))
         from_plane(s, 16, p_sem).wait_recv()
         span = pl.ds(PLACE[s], width)
         total = acc[coord[order[1]], :, cols(base + coord[order[0]] * width, width)]
@@ -255,14 +265,6 @@
             ))
             axis3[-1].start()
 
-    copies_n = []
-    for step in range(1, DET):
-        to = lax.rem(det + step, DET)
-        copies_n.append(
-            remote(cnt.at[to], cnt_got.at[step - 1], t_sem.at[0], t_sem.at[1], (wafer, to))
-        )
-        copies_n[-1].start()
-
     for s, (base, width, order) in enumerate(SETS):
         for one in axis3[3 * s:3 * s + 3]:
             one.wait_recv()
@@ -274,6 +276,11 @@
         for p, q in steps:
             remote(here, here, g_sem.at[s, 0], g_sem.at[s, 1], reach({order[0]: p, order[1]: q})).start()
 
+    def send_counts():
+        for step in range(1, DET):
+            to = lax.rem(det + step, DET)
+            remote(cnt.at[to], cnt_got.at[step - 1], t_sem.at[0], t_sem.at[1], (wafer, to)).start()
+
     def model_block(b, wide):
         span = cols(b * 512, 512)
         a_hi, a_lo = split(amp[:, :, span].reshape(MODES, 512))
@@ -281,19 +288,35 @@
         model[:, span] = value[0:ROWS]
         return choose(b, value[ROWS:ROWS + CROSS], wide)
 
+    def resid_blocks(side, g):
+        for b in range(WIDE // CHUNK):
+            first = side * HALF + g * WIDE + b * CHUNK
+            span = cols(first, CHUNK)
+            r_hi, r_lo = split(jnp.where(mask[:, span] != 0, tod[:, span] - model[:, span], 0.0))
+            res_hi[:, cols(first + 128, CHUNK)] = r_hi
+            res_lo[:, cols(first + 128, CHUNK)] = r_lo
+
+    def model_blocks(side, g, wide):
+        for b in range(WIDE // CHUNK):
+            wide = model_block((side * HALF + g * WIDE) // CHUNK + b, wide)
+        return wide
+
     wide = no_tiles
     copies_a = []
-    for s, (base, width, _) in enumerate(SETS):
-        from_plane(s, 8, g_sem).wait_recv()
-        half = amp.at[:, :, cols(core * HALF + base, RING * width)]
-        copies_a.append(remote(half, half, gc_sem.at[s, 0], gc_sem.at[s, 1], partner))
-        copies_a[-1].start()
-        first = core * (HALF // 512) + base // 512
-        wide = lax.fori_loop(first, first + RING * width // 512, model_block, wide)
-    for s, (base, width, _) in enumerate(SETS):
-        copies_a[s].wait_recv()
-        first = (1 - core) * (HALF // 512) + base // 512
-        wide = lax.fori_loop(first, first + RING * width // 512, model_block, wide)
+    for g, members in enumerate(GROUPS):
+        for s in members:
+            from_plane(s, 8, g_sem).wait_recv()
+        half = amp.at[:, :, cols(core * HALF + g * WIDE, WIDE)]
+        copies_a.append(remote(half, half, gc_sem.at[g, 0], gc_sem.at[g, 1], partner))
+        copies_a[g].start()
+        if g == len(GROUPS) - 1:
+            send_counts()
+        wide = model_blocks(core, g, wide)
+        resid_blocks(core, g)
+        if g > 0:
+            resid_blocks(1 - core, g - 1)
+        copies_a[g].wait_recv()
+        wide = model_blocks(1 - core, g, wide)
 
     rows = jnp.where(good_snip[...] != 0.0, tod_snip[...] - shifted(wide), 0.0)
     snip[0:CROSS, :] = rows[:, 0:128]
@@ -308,14 +331,7 @@
         )
         copies_t[-1].start()
 
-    def resid_block(b, carry):
-        span = cols(b * 512, 512)
-        r_hi, r_lo = split(jnp.where(mask[:, span] != 0, tod[:, span] - model[:, span], 0.0))
-        res_hi[:, cols(b * 512 + 128, 512)] = r_hi
-        res_lo[:, cols(b * 512 + 128, 512)] = r_lo
-        return carry
-
-    lax.fori_loop(0, NS // 512, resid_block, 0)
+    resid_blocks(1 - core, len(GROUPS) - 1)
     lane64 = lax.broadcasted_iota(jnp.int32, (ROWS, 128), 1) < 64
 
     def fill_block(b, carry):
@@ -360,7 +376,7 @@
 
     for one in copies_c + copies_a + axis3:
         one.wait_send()
-    for s in range(3):
+    for s in range(len(SETS)):
         from_plane(s, 16, p_sem).wait_send()
         from_plane(s, 8, g_sem).wait_send()
 
@@ -417,14 +433,14 @@
             pltpu.VMEM((DET, 8, 128), F32),
             pltpu.VMEM((DET, 8, 128), F32),
             pltpu.VMEM((DET, 8, 128), F32),
-            pltpu.SemaphoreType.DMA((2, 3, 2)),
+            pltpu.SemaphoreType.DMA((2, 2, 2)),
             pltpu.SemaphoreType.DMA((6,)),
             pltpu.SemaphoreType.REGULAR,
-            pltpu.SemaphoreType.DMA((3, 2)),
-            pltpu.SemaphoreType.DMA((3, 2)),
-            pltpu.SemaphoreType.DMA((3, 3, 2)),
-            pltpu.SemaphoreType.DMA((3, 2)),
-            pltpu.SemaphoreType.DMA((3, 2)),
+            pltpu.SemaphoreType.DMA((2, 2)),
+            pltpu.SemaphoreType.DMA((6, 2)),
+            pltpu.SemaphoreType.DMA((6, 3, 2)),
+            pltpu.SemaphoreType.DMA((6, 2)),
+            pltpu.SemaphoreType.DMA((2, 2)),
             pltpu.SemaphoreType.DMA((4,)),
         ],
         compiler_params=pltpu.CompilerParams(

time: 42.5 us -> 40.6 us (0.955)
  Pallas kernels: 41.7 us -> 39.8 us
    pallas_call x1, Pallas kernels: 40.4 us -> 38.5 us  [on_device(): pl.pallas_call(kernel, out_shape=shapes, in_specs=[hbm] * 8, out_specs=(v...]
where the time goes in v5:
time: 40.6 us; the launch traced here: 40.5 us
  Pallas kernels  39.8 us (98%)
  between operations  0.64 us (2%)
    pallas_call x1, Pallas kernels, on_device(): pl.pallas_call(kernel, out_shape=shapes, in_specs=[hbm] * 8, out_specs=(v...  38.5 us
    pallas_call x1, Pallas kernels, on_device(): pl.pallas_call(hand_out, out_shape=shapes, in_specs=[vmem] * 2, out_specs...  1.34 us

profile of v5, /device:TPU:1, one launch (start us, length us, event | category | flops | bytes accessed | tf_op | source)
XLA Modules:
  0.0 40.5 jit_solution(6078710952311928922)
XLA Ops:
  0.6 38.5 %shard_map.95 = (f32[64,8192]{1,0:T(8,128)S(1)}, f32[1,4,256]{2,1,0:T(4,128)S(1)}) custom-call(f32[64,8192]{1,0:T(8,128)} %tod_hbm.1, s32[64,8192]{1,0:T(8,128)} %mask_hbm.1, f32[32,64]{1,0:T(8,128)} %bitcast.6, f32[1,129]{1,0:T(1,128)} %bitcast.7, s32[1,64]{1,0:T(1,128)} %bitcast.8, s32[1,64]{1,0:T(1,128)} %bitcast.9, s32[1,64]{1,0:T(1,128)} %bitcast.10, ...), custom_call_target="tpu_custom_call" | custom-call | tf_op jit(solution)/shard_map/pallas_call | solution.py:398
  39.1 1.3 %shard_map.96 = (f32[64,8192]{1,0:T(8,128)}, f32[1,4,256]{2,1,0:T(4,128)}) custom-call(f32[64,8192]{1,0:T(8,128)S(1)} %get-tuple-element.4.filled, f32[1,4,256]{2,1,0:T(4,128)S(1)} %get-tuple-element.5.templ), custom_call_target="tpu_custom_call" | custom-call | tf_op jit(solution)/shard_map/pallas_call | solution.py:451

commit v6 on v5

--- a/solution.py
+++ b/solution.py
@@ -86,8 +86,8 @@
 
     halves = (1 - core, core)
     loads = {}
-    for h in range(2):
-        for g in range(len(GROUPS)):
+    for g in range(len(GROUPS)):
+        for h in range(2):
             span = cols(halves[h] * HALF + g * WIDE, WIDE)
             loads[h, g] = (
                 pltpu.make_async_copy(tod_hbm.at[:, span], tod.at[:, span], in_sem.at[h, g, 0]),
@@ -103,8 +103,6 @@
 
     small[0].wait()
     coup_t = coup_ref[...]
-    c_hi, c_lo = split(coup_t.T)
-    lhs_m[0:ROWS, :] = jnp.concatenate([c_hi, c_lo, c_hi], axis=1)
     t_hi, t_lo = split(coup_t)
     w_hi, w_lo = split(coup_t * coup_t)
     zero = jnp.zeros((MODES, ROWS), BF16)
@@ -134,7 +132,7 @@
                 dst[j, 8:16, span] = weights[8 * j:8 * j + 8]
             return carry
 
-        lax.fori_loop(0, WIDE // CHUNK, body, 0)
+        lax.fori_loop(0, WIDE // CHUNK, body, 0, unroll=True)
 
     copies_c = []
     for g in range(len(GROUPS)):
@@ -143,12 +141,12 @@
             remote(part.at[:, :, span], got_c.at[:, :, span], c_sem.at[g, 0], c_sem.at[g, 1], partner)
         )
     fill(0, 0, part)
-    fill(0, 1, part)
     pl.semaphore_wait(barrier, 1 + len(lines))
     copies_c[0].start()
     for to in lines:
         pl.semaphore_signal(ready_sem, inc=1, device_id=to, device_id_type=MESH)
     fill(1, 0, acc)
+    fill(0, 1, part)
     copies_c[1].start()
 
     steps = sorted(
@@ -176,10 +174,10 @@
     take(0)
     for s in GROUPS[0]:
         scatter(s, on_line)
+    fill(1, 1, acc)
     pl.semaphore_wait(ready_sem, len(lines))
     for s in GROUPS[0]:
         scatter(s, off_line)
-    fill(1, 1, acc)
     take(1)
     for s in GROUPS[1]:
         scatter(s, steps)
@@ -201,6 +199,8 @@
     start = jnp.broadcast_to(cstart_ref[...], (128, CROSS)).T
     first_tile[...] = start >> 7
     shift[...] = start & 127
+    c_hi, c_lo = split(coup_ref[...].T)
+    lhs_m[0:ROWS, :] = jnp.concatenate([c_hi, c_lo, c_hi], axis=1)
     lhs_m[ROWS:ROWS + CROSS, :] = dot(of_det, lhs_m[0:ROWS, :]).astype(BF16)
     cnt[...] = jnp.broadcast_to(jnp.sum(oh_t, axis=1, keepdims=True), (256, 128)).reshape(DET, 8, 128)
 
@@ -217,7 +217,8 @@
         wide = list(wide)
         for q in range(4):
             for w in range(3):
-                wide[w] = jnp.where(at[q - w], lines[:, 128 * q:128 * q + 128], wide[w])
+                for k, line in enumerate(lines):
+                    wide[3 * k + w] = jnp.where(at[q - w], line[:, 128 * q:128 * q + 128], wide[3 * k + w])
         return tuple(wide)
 
     def shifted(wide):
@@ -230,16 +231,17 @@
 
     no_tiles = (jnp.zeros((CROSS, 128), F32),) * 3
 
-    def tod_block(b, wide):
+    def input_block(b, wide):
         span = cols(b * 512, 512)
-        v_hi, v_lo = split(jnp.where(mask[:, span] != 0, tod[:, span], 0.0))
-        return choose(b, dot(dets[...], jnp.concatenate([v_hi, v_lo], axis=0)), wide)
-
-    def good_block(b, wide):
-        g = mask[:, cols(b * 512, 512)].astype(F32).astype(BF16)
-        return choose(b, dot(dets[:, 0:ROWS], g), wide)
-
-    tod_snip[...] = shifted(lax.fori_loop(0, NS // 512, tod_block, no_tiles))
+        m = mask[:, span]
+        v_hi, v_lo = split(jnp.where(m != 0, tod[:, span], 0.0))
+        g = m.astype(F32).astype(BF16)
+        lines = dot(dets[...], jnp.concatenate([v_hi, v_lo], axis=0)), dot(dets[:, 0:ROWS], g)
+        return choose(b, lines, wide)
+
+    inputs = lax.fori_loop(0, NS // 512, input_block, no_tiles * 2)
+    tod_snip[...] = shifted(inputs[0:3])
+    good_snip[...] = shifted(inputs[3:6])
     for edge in (res_hi, res_lo):
         edge[:, 0:128] = jnp.zeros((ROWS, 128), BF16)
         edge[:, 128 + NS:256 + NS] = jnp.zeros((ROWS, 128), BF16)
@@ -250,8 +252,6 @@
 
     axis3 = []
     for s, (base, width, order) in enumerate(SETS):
-        if s == GROUPS[1][0]:
-            good_snip[...] = shifted(lax.fori_loop(0, NS // 512, good_block, no_tiles))
         from_plane(s, 16, p_sem).wait_recv()
         span = pl.ds(PLACE[s], width)
         total = acc[coord[order[1]], :, cols(base + coord[order[0]] * width, width)]
@@ -276,17 +276,23 @@
         for p, q in steps:
             remote(here, here, g_sem.at[s, 0], g_sem.at[s, 1], reach({order[0]: p, order[1]: q})).start()
 
-    def send_counts():
-        for step in range(1, DET):
-            to = lax.rem(det + step, DET)
-            remote(cnt.at[to], cnt_got.at[step - 1], t_sem.at[0], t_sem.at[1], (wafer, to)).start()
+    owners = []
+    for p, q in steps + [(0, 0)]:
+        for other in (0, 1):
+            if p or q or other:
+                at = reach({"x": p, "y": q})[1]
+                owners.append(at + other * (1 - 2 * core))
+
+    def to_owners(src, dst, send, recv):
+        for k, to in enumerate(owners):
+            remote(src.at[to], dst.at[k], send, recv, (wafer, to)).start()
 
     def model_block(b, wide):
         span = cols(b * 512, 512)
         a_hi, a_lo = split(amp[:, :, span].reshape(MODES, 512))
         value = dot(lhs_m[...], jnp.concatenate([a_hi, a_hi, a_lo], axis=0))
         model[:, span] = value[0:ROWS]
-        return choose(b, value[ROWS:ROWS + CROSS], wide)
+        return choose(b, (value[ROWS:ROWS + CROSS],), wide)
 
     def resid_blocks(side, g):
         for b in range(WIDE // CHUNK):
@@ -309,9 +315,9 @@
         half = amp.at[:, :, cols(core * HALF + g * WIDE, WIDE)]
         copies_a.append(remote(half, half, gc_sem.at[g, 0], gc_sem.at[g, 1], partner))
         copies_a[g].start()
-        if g == len(GROUPS) - 1:
-            send_counts()
         wide = model_blocks(core, g, wide)
+        if g == 0:
+            to_owners(cnt, cnt_got, t_sem.at[0], t_sem.at[1])
         resid_blocks(core, g)
         if g > 0:
             resid_blocks(1 - core, g - 1)
@@ -323,13 +329,7 @@
     snip[CROSS:2 * CROSS, :] = rows[:, 128:256]
     s_hi, s_lo = split(snip[...])
     tsum[...] = dot(slots[...], jnp.concatenate([s_hi, s_lo], axis=0)).reshape(DET, 8, 128)
-    copies_t = []
-    for step in range(1, DET):
-        to = lax.rem(det + step, DET)
-        copies_t.append(
-            remote(tsum.at[to], tsum_got.at[step - 1], t_sem.at[2], t_sem.at[3], (wafer, to))
-        )
-        copies_t[-1].start()
+    to_owners(tsum, tsum_got, t_sem.at[2], t_sem.at[3])
 
     resid_blocks(1 - core, len(GROUPS) - 1)
     lane64 = lax.broadcasted_iota(jnp.int32, (ROWS, 128), 1) < 64
@@ -362,30 +362,31 @@
         every.wait_recv()
         every.wait_send()
 
-    wait_all(cnt, cnt_got, t_sem.at[0], t_sem.at[1])
-    wait_all(tsum, tsum_got, t_sem.at[2], t_sem.at[3])
-    number = cnt[det]
-    total = tsum[det]
-    for step in range(DET - 1):
-        number += cnt_got[step]
-        total += tsum_got[step]
-    snip[0:8, :] = total / (number + 1.0)
-    for o in range(4):
-        templ_ref[0, o:o + 1, 0:128] = snip[2 * o:2 * o + 1, :]
-        templ_ref[0, o:o + 1, 128:256] = snip[2 * o + 1:2 * o + 2, :]
-
     for one in copies_c + copies_a + axis3:
         one.wait_send()
     for s in range(len(SETS)):
         from_plane(s, 16, p_sem).wait_send()
         from_plane(s, 8, g_sem).wait_send()
 
+    wait_all(cnt, cnt_got, t_sem.at[0], t_sem.at[1])
+    number = cnt[det]
+    for k in range(DET - 1):
+        number += cnt_got[k]
+    wait_all(tsum, tsum_got, t_sem.at[2], t_sem.at[3])
+    total = tsum[det]
+    for k in range(DET - 1):
+        total += tsum_got[k]
+    snip[0:8, :] = total / (number + 1.0)
+    for o in range(4):
+        templ_ref[0, o:o + 1, 0:128] = snip[2 * o:2 * o + 1, :]
+        templ_ref[0, o:o + 1, 128:256] = snip[2 * o + 1:2 * o + 2, :]
+
 
 def hand_out(filled, templ, filled_out, templ_out, sem):
-    copies = [
-        pltpu.make_async_copy(filled, filled_out, sem.at[0]),
-        pltpu.make_async_copy(templ, templ_out, sem.at[1]),
-    ]
+    copies = [pltpu.make_async_copy(templ, templ_out, sem.at[8])]
+    for k in range(8):
+        strip = pl.ds(8 * k, 8)
+        copies.append(pltpu.make_async_copy(filled.at[strip], filled_out.at[strip], sem.at[k]))
     for one in copies:
         one.start()
     for one in copies:
@@ -453,7 +454,7 @@
         out_shape=shapes,
         in_specs=[vmem] * 2,
         out_specs=(hbm, hbm),
-        scratch_shapes=[pltpu.SemaphoreType.DMA((2,))],
+        scratch_shapes=[pltpu.SemaphoreType.DMA((9,))],
         compiler_params=pltpu.CompilerParams(vmem_limit_bytes=1 << 20),
     )(*results)
 

time: 40.6 us -> 39.3 us (0.968)
  Pallas kernels: 39.8 us -> 38.4 us
    pallas_call x1, Pallas kernels: 38.5 us -> 37.1 us  [on_device(): pl.pallas_call(kernel, out_shape=shapes, in_specs=[hbm] * 8, out_specs=(v...]
where the time goes in v6:
time: 39.3 us; the launch traced here: 39.1 us
  Pallas kernels  38.4 us (98%)
  between operations  0.64 us (2%)
    pallas_call x1, Pallas kernels, on_device(): pl.pallas_call(kernel, out_shape=shapes, in_specs=[hbm] * 8, out_specs=(v...  37.1 us
    pallas_call x1, Pallas kernels, on_device(): pl.pallas_call(hand_out, out_shape=shapes, in_specs=[vmem] * 2, out_specs...  1.39 us

profile of v6, /device:TPU:1, one launch (start us, length us, event | category | flops | bytes accessed | tf_op | source)
XLA Modules:
  0.0 39.1 jit_solution(9158892080755875128)
XLA Ops:
  0.6 37.1 %shard_map.95 = (f32[64,8192]{1,0:T(8,128)S(1)}, f32[1,4,256]{2,1,0:T(4,128)S(1)}) custom-call(f32[64,8192]{1,0:T(8,128)} %tod_hbm.1, s32[64,8192]{1,0:T(8,128)} %mask_hbm.1, f32[32,64]{1,0:T(8,128)} %bitcast.6, f32[1,129]{1,0:T(1,128)} %bitcast.7, s32[1,64]{1,0:T(1,128)} %bitcast.8, s32[1,64]{1,0:T(1,128)} %bitcast.9, s32[1,64]{1,0:T(1,128)} %bitcast.10, ...), custom_call_target="tpu_custom_call" | custom-call | tf_op jit(solution)/shard_map/pallas_call | solution.py:399
  37.7 1.4 %shard_map.96 = (f32[64,8192]{1,0:T(8,128)}, f32[1,4,256]{2,1,0:T(4,128)}) custom-call(f32[64,8192]{1,0:T(8,128)S(1)} %get-tuple-element.4.filled, f32[1,4,256]{2,1,0:T(4,128)S(1)} %get-tuple-element.5.templ), custom_call_target="tpu_custom_call" | custom-call | tf_op jit(solution)/shard_map/pallas_call | solution.py:452

commit v7 on v6

--- a/solution.py
+++ b/solution.py
@@ -172,15 +172,18 @@
         acc[:, :, span] += got_c[:, :, span]
 
     take(0)
-    for s in GROUPS[0]:
-        scatter(s, on_line)
+    for v in on_line:
+        for s in GROUPS[0]:
+            scatter(s, [v])
     fill(1, 1, acc)
     pl.semaphore_wait(ready_sem, len(lines))
-    for s in GROUPS[0]:
-        scatter(s, off_line)
+    for v in off_line:
+        for s in GROUPS[0]:
+            scatter(s, [v])
     take(1)
-    for s in GROUPS[1]:
-        scatter(s, steps)
+    for v in steps:
+        for s in GROUPS[1]:
+            scatter(s, [v])
 
     for one in small[2:]:
         one.wait()

time: 39.3 us -> 39.1 us (level)
  no operation moved by 1% of the time
where the time goes in v7:
time: 39.1 us; the launch traced here: 38.9 us
  Pallas kernels  38.2 us (98%)
  between operations  0.64 us (2%)
    pallas_call x1, Pallas kernels, on_device(): pl.pallas_call(kernel, out_shape=shapes, in_specs=[hbm] * 8, out_specs=(v...  36.8 us
    pallas_call x1, Pallas kernels, on_device(): pl.pallas_call(hand_out, out_shape=shapes, in_specs=[vmem] * 2, out_specs...  1.39 us

profile of v7, /device:TPU:1, one launch (start us, length us, event | category | flops | bytes accessed | tf_op | source)
XLA Modules:
  0.0 38.9 jit_solution(16984626431532077813)
XLA Ops:
  0.6 36.8 %shard_map.95 = (f32[64,8192]{1,0:T(8,128)S(1)}, f32[1,4,256]{2,1,0:T(4,128)S(1)}) custom-call(f32[64,8192]{1,0:T(8,128)} %tod_hbm.1, s32[64,8192]{1,0:T(8,128)} %mask_hbm.1, f32[32,64]{1,0:T(8,128)} %bitcast.6, f32[1,129]{1,0:T(1,128)} %bitcast.7, s32[1,64]{1,0:T(1,128)} %bitcast.8, s32[1,64]{1,0:T(1,128)} %bitcast.9, s32[1,64]{1,0:T(1,128)} %bitcast.10, ...), custom_call_target="tpu_custom_call" | custom-call | tf_op jit(solution)/shard_map/pallas_call | solution.py:402
  37.5 1.4 %shard_map.96 = (f32[64,8192]{1,0:T(8,128)}, f32[1,4,256]{2,1,0:T(4,128)}) custom-call(f32[64,8192]{1,0:T(8,128)S(1)} %get-tuple-element.4.filled, f32[1,4,256]{2,1,0:T(4,128)S(1)} %get-tuple-element.5.templ), custom_call_target="tpu_custom_call" | custom-call | tf_op jit(solution)/shard_map/pallas_call | solution.py:455

commit v8 on v7

--- a/solution.py
+++ b/solution.py
@@ -268,16 +268,21 @@
             ))
             axis3[-1].start()
 
-    for s, (base, width, order) in enumerate(SETS):
-        for one in axis3[3 * s:3 * s + 3]:
-            one.wait_recv()
-        span = pl.ds(PLACE[s], width)
-        whole = (acc2[:, span] + got3[0, :, span]) + (got3[1, :, span] + got3[2, :, span])
-        block = cols(core * HALF + base + coord[order[0]] * width, width)
-        amp[coord[order[1]], :, block] = whole[0:8] / (whole[8:16] + 1.0)
-        here = amp.at[coord[order[1]], :, block]
+    for members in GROUPS:
+        here = {}
+        for s in members:
+            base, width, order = SETS[s]
+            for one in axis3[3 * s:3 * s + 3]:
+                one.wait_recv()
+            span = pl.ds(PLACE[s], width)
+            whole = (acc2[:, span] + got3[0, :, span]) + (got3[1, :, span] + got3[2, :, span])
+            block = cols(core * HALF + base + coord[order[0]] * width, width)
+            amp[coord[order[1]], :, block] = whole[0:8] / (whole[8:16] + 1.0)
+            here[s] = amp.at[coord[order[1]], :, block]
         for p, q in steps:
-            remote(here, here, g_sem.at[s, 0], g_sem.at[s, 1], reach({order[0]: p, order[1]: q})).start()
+            for s in members:
+                to = reach({SETS[s][2][0]: p, SETS[s][2][1]: q})
+                remote(here[s], here[s], g_sem.at[s, 0], g_sem.at[s, 1], to).start()
 
     owners = []
     for p, q in steps + [(0, 0)]:

time: 39.1 us -> 39.2 us (level)
  no operation moved by 1% of the time
where the time goes in v8:
time: 39.2 us; the launch traced here: 39 us
  Pallas kernels  38.3 us (98%)
  between operations  0.64 us (2%)
    pallas_call x1, Pallas kernels, on_device(): pl.pallas_call(kernel, out_shape=shapes, in_specs=[hbm] * 8, out_specs=(v...  36.9 us
    pallas_call x1, Pallas kernels, on_device(): pl.pallas_call(hand_out, out_shape=shapes, in_specs=[vmem] * 2, out_specs...  1.39 us

profile of v8, /device:TPU:1, one launch (start us, length us, event | category | flops | bytes accessed | tf_op | source)
XLA Modules:
  0.0 39.0 jit_solution(5621419645697208581)
XLA Ops:
  0.6 36.9 %shard_map.95 = (f32[64,8192]{1,0:T(8,128)S(1)}, f32[1,4,256]{2,1,0:T(4,128)S(1)}) custom-call(f32[64,8192]{1,0:T(8,128)} %tod_hbm.1, s32[64,8192]{1,0:T(8,128)} %mask_hbm.1, f32[32,64]{1,0:T(8,128)} %bitcast.6, f32[1,129]{1,0:T(1,128)} %bitcast.7, s32[1,64]{1,0:T(1,128)} %bitcast.8, s32[1,64]{1,0:T(1,128)} %bitcast.9, s32[1,64]{1,0:T(1,128)} %bitcast.10, ...), custom_call_target="tpu_custom_call" | custom-call | tf_op jit(solution)/shard_map/pallas_call | solution.py:407
  37.6 1.4 %shard_map.96 = (f32[64,8192]{1,0:T(8,128)}, f32[1,4,256]{2,1,0:T(4,128)}) custom-call(f32[64,8192]{1,0:T(8,128)S(1)} %get-tuple-element.4.filled, f32[1,4,256]{2,1,0:T(4,128)S(1)} %get-tuple-element.5.templ), custom_call_target="tpu_custom_call" | custom-call | tf_op jit(solution)/shard_map/pallas_call | solution.py:460
